TPU v7x, 32 devices: a whole 2x2x4 slice. The times are simulated.
32 devices in a mesh: row: 2 (over x), col: 16 (over z, y, core).
Axes of the slice: x: 2, y: 2, z: 4, core: 2. Of those that a mesh axis runs over, the one named last changes fastest.
Arguments:
- coords: float32 [64, 3, 256], P(('row', 'col')), may hold values from 0 to 8, as said below
- noise_var: float32 [64, 256], P(('row', 'col')), may hold values from 0.1 to 1
- right_side: float32 [64, 8, 256], P(('row', 'col')), may hold values from -32 to 32
- start_guess: float32 [64, 8, 256], P(('row', 'col')), may hold values from -3 to 3
- tile_pairs: int32 [2, 16, 2, 63], P('row', 'col'), may hold values from -1 to 31, as said below
Outputs:
- solution_field: float32 [64, 8, 256], P(('row', 'col'))
- residual: float32 [64, 8, 256], P(('row', 'col'))
Inputs may be any that keep to these rules, and one draw needn't show every extreme that they name: `coords`: each tile's points lie within one unit cell of the integer lattice, and distinct tiles lie in distinct cells. `tile_pairs`: each device's list holds every pair of its block whose cells differ by at most one in each coordinate, each pair once and no other; listed entries come first, then entries of -1 in both rows.
All inputs are finite; a program needn't handle non-finite values.
Results may differ from a plain program's by a relative error of at most 0.0003.
Values sent between devices are 32-bit elements; how exact they have to be, the bound alone decides.
A program may use at most 64 MiB of HBM per device.

v0:
```python
import functools

import jax
import jax.numpy as jnp
from jax import lax
from jax.experimental import pallas as pl
from jax.experimental.pallas import tpu as pltpu
from jax.sharding import PartitionSpec as P

ITERS = 3
GROUP = 4
NEAR = 27
CAPACITY = -(-NEAR // GROUP) * GROUP
CORES = 2
MESH = pl.DeviceIdType.MESH
VMEM_SPEC = pl.BlockSpec(memory_space=pltpu.VMEM)
SMEM_SPEC = pl.BlockSpec(memory_space=pltpu.SMEM)
ANY_SPEC = pl.BlockSpec(memory_space=pl.ANY)


def factors(mesh_shape):
    rows, cols = mesh_shape
    chips = cols // CORES
    wide = 1
    while wide * wide * 4 <= chips:
        wide *= 2
    return rows, chips // wide, wide, CORES


def position(dims):
    xs, zs, ys, cs = dims
    x = lax.axis_index("row")
    col = lax.axis_index("col")
    return x, col // (ys * cs), (col // cs) % ys, col % cs


def flip(index, k, size):
    if size & (size - 1):
        return (k - index + 2 * size) % size
    result, bit = 0, 1
    while bit < size:
        result = result + (index // bit + k // bit) % 2 * bit
        bit *= 2
    return result


def gather_partners(dims):
    xs, zs, ys, cs = dims
    x, z, y, c = position(dims)
    partners = [(x, (((z + k) % zs) * ys + y) * cs + c) for k in range(1, zs)]
    if xs == 2 and ys == 2:
        partners += [(1 - x, (z * ys + 1 - y) * cs + c)]
    partners += [(x, (z * ys + (y + k) % ys) * cs + c) for k in range(1, ys)]
    partners += [((x + k) % xs, (z * ys + y) * cs + c) for k in range(1, xs)]
    partners += [(x, (z * ys + y) * cs + 1 - c)]
    return partners


def gather(dims, ins, outs, send_sem, recv_sem, local_sem):
    xs, zs, ys, cs = dims
    count = len(ins)
    x, z, y, c = position(dims)

    def device(xx, zz, yy, cc):
        return (xx, (zz * ys + yy) * cs + cc)

    def slot(xx, zz, yy, cc):
        return ((xx * zs + zz) * ys + yy) * cs + cc

    local = []
    for a in range(count):
        copy = pltpu.make_async_copy(ins[a], outs[a].at[slot(x, z, y, c)], local_sem.at[a])
        copy.start()
        local.append(copy)

    numbers = iter(range(10**6))
    sent = []

    def send(a, source, place, target):
        number = next(numbers)
        copy = pltpu.make_async_remote_copy(
            src_ref=source,
            dst_ref=outs[a].at[place],
            send_sem=send_sem.at[number],
            recv_sem=recv_sem.at[number],
            device_id=target,
            device_id_type=MESH,
        )
        copy.start()
        sent.append(copy)
        return copy

    mine = slot(x, z, y, c)
    other = device(x, z, y, 1 - c)
    along_z = {}
    for k in reversed(range(1, zs)):
        for a in range(count):
            along_z[k, a] = send(a, ins[a], mine, device(x, flip(z, k, zs), y, c))
    yield
    for a in range(count):
        local[a].wait()

    if xs == 2 and ys == 2:
        across_by = ((1 - x, 1 - y), ((x + c) % 2, (y + 1 - c) % 2), ((x + 1 - c) % 2, (y + c) % 2))
        arrivals, swaps = [], []
        for k in range(zs):
            level = flip(z, k, zs)
            for a in range(count):
                if k:
                    along_z[k, a].wait_recv()
                place = slot(x, level, y, c)
                for xx, yy in across_by:
                    copy = send(a, outs[a].at[place], place, device(xx, z, yy, c))
                    arrivals.append((copy, a, slot(xx, level, yy, c)))
                swaps.append(send(a, outs[a].at[place], place, other))
        yield
        for number, way in enumerate((1, 2, 0)):
            for copy, a, place in arrivals[way::3]:
                copy.wait_recv()
                swaps.append(send(a, outs[a].at[place], place, other))
            if number == 1:
                yield
        for copy in swaps:
            copy.wait_recv()
        for copy in sent:
            copy.wait_send()
        return

    def across(places, targets):
        for place in places:
            for a in range(count):
                for target in targets:
                    send(a, outs[a].at[place], place, target)

    def settle():
        for copy in sent:
            copy.wait()
        del sent[:]

    settle()
    across(
        [slot(x, zz, y, c) for zz in range(zs)],
        [device(x, z, (y + k) % ys, c) for k in range(1, ys)],
    )
    settle()
    across(
        [slot(x, zz, yy, c) for zz in range(zs) for yy in range(ys)],
        [device((x + k) % xs, z, y, c) for k in range(1, xs)],
    )
    settle()
    across(
        [slot(xx, zz, yy, c) for xx in range(xs) for zz in range(zs) for yy in range(ys)],
        [other],
    )
    settle()


def gather_kernel(dims, *refs):
    in_ref, out_ref, send_sem, recv_sem, local_sem = refs
    partners = gather_partners(dims)
    barrier = pltpu.get_barrier_semaphore()
    for partner in partners:
        pl.semaphore_signal(barrier, inc=1, device_id=partner, device_id_type=MESH)
    pl.semaphore_wait(barrier, len(partners))
    for _ in gather(dims, [in_ref], [out_ref], send_sem, recv_sem, local_sem):
        pass


def all_gather(dims, collective_id, slab):
    devices = dims[0] * dims[1] * dims[2] * dims[3]
    return pl.pallas_call(
        functools.partial(gather_kernel, dims),
        out_shape=jax.ShapeDtypeStruct((devices,) + slab.shape, slab.dtype),
        in_specs=[VMEM_SPEC],
        out_specs=VMEM_SPEC,
        scratch_shapes=[
            pltpu.SemaphoreType.DMA((devices - 1,)),
            pltpu.SemaphoreType.DMA((devices - 1,)),
            pltpu.SemaphoreType.DMA((1,)),
        ],
        compiler_params=pltpu.CompilerParams(collective_id=collective_id, has_side_effects=True),
    )(slab)


def split_rows(values):
    high = values.astype(jnp.bfloat16)
    low = (values - high.astype(jnp.float32)).astype(jnp.bfloat16)
    return jnp.concatenate([high, low], axis=0)


def solve_kernel(
    dims, groups,
    near_ref, side_ref, points_ref, own_points_ref, noise_ref, right_ref, guess_ref,
    field_out, residual_out,
    buffers, dir_ref, vectors_ref, blocks, outgoing, dot_ref, dots_ref,
    send_sem, recv_sem, local_sem, dot_send, dot_recv,
):
    cols = dims[1] * dims[2] * dims[3]
    devices = dims[0] * cols
    tiles, tile = points_ref.shape[0], points_ref.shape[2]
    own, rhs, _ = right_ref.shape
    me = lax.axis_index("row") * cols + lax.axis_index("col")

    def peer(k):
        number = (me + k) % devices
        return (number // cols, number % cols)

    barrier = pltpu.get_barrier_semaphore()

    def greet(k, carry):
        pl.semaphore_signal(barrier, inc=1, device_id=peer(k), device_id_type=MESH)
        return carry

    lax.fori_loop(1, devices, greet, 0)

    def spreading(number, source):
        return gather(
            dims, [source], [buffers.at[number]],
            send_sem.at[number], recv_sem.at[number], local_sem.at[number],
        )

    def spread(number, source):
        for _ in spreading(number, source):
            pass

    rows = 32
    block = 2 * tile

    def build(e, carry):
        left = points_ref[jnp.maximum(near_ref[e], 0)].T
        right = own_points_ref[side_ref[e // GROUP]]
        reach = jnp.minimum(near_ref[e] + 1, 1).astype(jnp.float32)
        for chunk in range(tile // rows):
            squared = None
            for component in range(3):
                spacing = (
                    left[chunk * rows : (chunk + 1) * rows, component : component + 1]
                    - right[component : component + 1, :]
                )
                term = spacing * spacing
                squared = term if squared is None else squared + term
            distance = squared * lax.rsqrt(jnp.maximum(squared, 1e-30))
            remain = jnp.maximum(reach - distance, 0.0)
            remain = remain * remain
            weights = remain * remain * (4.0 * distance + 1.0)
            high = weights.astype(jnp.bfloat16)
            low = (weights - high.astype(jnp.float32)).astype(jnp.bfloat16)
            at = pl.multiple_of(e * block + chunk * rows, rows)
            blocks[pl.ds(at, rows), :] = high
            at = pl.multiple_of(e * block + tile + chunk * rows, rows)
            blocks[pl.ds(at, rows), :] = low
        return carry

    def image_of():
        def step(g, totals):
            parts = []
            for i in range(GROUP):
                part = vectors_ref[jnp.maximum(near_ref[g * GROUP + i], 0)]
                parts += [part, part]
            first = pl.multiple_of(g * GROUP * block, GROUP * block)
            term = jnp.dot(
                jnp.concatenate(parts, axis=1),
                blocks[pl.ds(first, GROUP * block), :],
                preferred_element_type=jnp.float32,
            )
            place = side_ref[g].astype(jnp.float32)
            return tuple(
                total + term * jnp.maximum(1.0 - jnp.abs(place - float(p)), 0.0)
                for p, total in enumerate(totals)
            )

        start = tuple(jnp.zeros((2 * rhs, tile), jnp.float32) for _ in range(own))
        totals = lax.fori_loop(0, groups, step, start, unroll=4 if groups % 4 == 0 else 2)
        return [total[:rhs] + total[rhs:] for total in totals]

    def over_tiles(body, start):
        def one(i, carry):
            return body(i // own, i % own, carry)

        return lax.fori_loop(0, tiles, one, start, unroll=16)

    zero = jnp.zeros((rhs, tile), jnp.float32)
    noise = [noise_ref[p : p + 1, :] for p in range(own)]

    shares = 5
    bounds = [groups * GROUP // 2 * i // shares * 2 for i in range(shares + 1)]
    lax.fori_loop(bounds[0], bounds[1], build, 0, unroll=2)
    pl.semaphore_wait(barrier, devices - 1)
    built = 1
    for _ in spreading(0, guess_ref):
        lax.fori_loop(bounds[built], bounds[built + 1], build, 0, unroll=2)
        built += 1
    lax.fori_loop(bounds[built], bounds[shares], build, 0, unroll=2)

    def take_guess(i, p, carry):
        vectors_ref[i * own + p] = split_rows(buffers[0, i, p])
        return carry

    over_tiles(take_guess, 0)
    for p, image in enumerate(image_of()):
        outgoing[0, p] = right_ref[p] - (image + noise[p] * guess_ref[p])
    spread(1, outgoing.at[0])

    def take_residual(i, p, total):
        value = buffers[1, i, p]
        dir_ref[i, p] = value
        vectors_ref[i * own + p] = split_rows(value)
        return total + value * value

    norm = jnp.sum(over_tiles(take_residual, zero), axis=1, keepdims=True)
    for p in range(own):
        field_out[p] = guess_ref[p]
    for iteration in range(1, ITERS):
        for p, image in enumerate(image_of()):
            outgoing[iteration, p] = image + noise[p] * dir_ref[me, p]
        spread(1 + iteration, outgoing.at[iteration])

        def dots(i, p, total):
            return total + dir_ref[i, p] * buffers[1 + iteration, i, p]

        inner = jnp.sum(over_tiles(dots, zero), axis=1, keepdims=True)
        step_size = norm / inner
        for p in range(own):
            field_out[p] = field_out[p] + step_size * dir_ref[me, p]

        def descend(i, p, total):
            value = buffers[1, i, p] - step_size * buffers[1 + iteration, i, p]
            buffers[1, i, p] = value
            return total + value * value

        norm_next = jnp.sum(over_tiles(descend, zero), axis=1, keepdims=True)
        turn = norm_next / norm

        def redirect(i, p, carry):
            value = buffers[1, i, p] + turn * dir_ref[i, p]
            dir_ref[i, p] = value
            vectors_ref[i * own + p] = split_rows(value)
            return carry

        over_tiles(redirect, 0)
        norm = norm_next

    images, total = [], zero
    for p, image in enumerate(image_of()):
        value = dir_ref[me, p]
        image = image + noise[p] * value
        images.append(image)
        total = total + value * image
    eye = lax.broadcasted_iota(jnp.int32, (rhs, 128), 0) == lax.broadcasted_iota(
        jnp.int32, (rhs, 128), 1
    )
    share = jnp.sum(total, axis=1, keepdims=True)
    row = jnp.sum(jnp.where(eye, share, 0.0), axis=0, keepdims=True)
    dot_ref[...] = row
    dots_ref[me] = row

    def dot_copy(k):
        return pltpu.make_async_remote_copy(
            src_ref=dot_ref,
            dst_ref=dots_ref.at[me],
            send_sem=dot_send.at[k],
            recv_sem=dot_recv.at[k],
            device_id=peer(k),
            device_id_type=MESH,
        )

    def start_dot(k, carry):
        dot_copy(k).start()
        return carry

    def wait_dot(k, carry):
        dot_copy(k).wait()
        return carry

    lax.fori_loop(1, devices, start_dot, 0)
    lax.fori_loop(1, devices, wait_dot, 0)
    inner = jnp.sum(dots_ref[...], axis=0)
    inner = jnp.sum(jnp.where(eye, inner, 0.0), axis=1, keepdims=True)
    step_size = norm / inner
    for p in range(own):
        field_out[p] = field_out[p] + step_size * dir_ref[me, p]
        residual_out[p] = buffers[1, me, p] - step_size * images[p]


def solve(dims, groups, collective_id, *operands):
    devices = dims[0] * dims[1] * dims[2] * dims[3]
    points, right = operands[2], operands[5]
    tiles, tile = points.shape[0], points.shape[2]
    own, rhs, _ = right.shape
    dma = pltpu.SemaphoreType.DMA
    phases = 1 + ITERS
    return pl.pallas_call(
        functools.partial(solve_kernel, dims, groups),
        out_shape=[jax.ShapeDtypeStruct(right.shape, jnp.float32)] * 2,
        in_specs=[SMEM_SPEC] * 2 + [VMEM_SPEC] * 5,
        out_specs=[VMEM_SPEC] * 2,
        scratch_shapes=[
            pltpu.VMEM((phases, devices, own, rhs, tile), jnp.float32),
            pltpu.VMEM((devices, own, rhs, tile), jnp.float32),
            pltpu.VMEM((tiles, 2 * rhs, tile), jnp.bfloat16),
            pltpu.VMEM((groups * GROUP * 2 * tile, tile), jnp.bfloat16),
            pltpu.VMEM((ITERS, own, rhs, tile), jnp.float32),
            pltpu.VMEM((1, 128), jnp.float32),
            pltpu.VMEM((devices, 1, 128), jnp.float32),
            dma((phases, devices - 1)),
            dma((phases, devices - 1)),
            dma((phases, 1)),
            dma((devices,)),
            dma((devices,)),
        ],
        compiler_params=pltpu.CompilerParams(
            collective_id=collective_id, has_side_effects=True, vmem_limit_bytes=60 * 2**20
        ),
    )(*operands)


def shards(mesh_shape, coords, noise_var, right_side, start_guess, tile_pairs):
    dims = factors(mesh_shape)
    devices = mesh_shape[0] * mesh_shape[1]
    own, _, tile = coords.shape
    tiles = own * devices
    me = lax.axis_index("row") * mesh_shape[1] + lax.axis_index("col")
    padded = jnp.pad(coords, ((0, 0), (0, 5), (0, 0)))
    points = all_gather(dims, 0, padded).reshape(tiles, 8, tile)

    low, high = jnp.min(points, axis=2), jnp.max(points, axis=2)
    gap = jnp.maximum(low[None] - high[:, None], low[:, None] - high[None])
    near = jnp.all(gap < 1.0, axis=2).astype(jnp.int32)
    needed = -(-jnp.sum(near, axis=1) // GROUP)
    largest = jnp.max(jnp.sum(needed.reshape(devices, own), axis=1))
    own_near = lax.dynamic_slice_in_dim(near, me * own, own)
    own_needed = lax.dynamic_slice_in_dim(needed, me * own, own)
    ids = jnp.arange(tiles, dtype=jnp.int32)
    rank = jnp.sum(own_near[:, None, :] * (ids[None, None, :] < ids[None, :, None]), axis=2)
    places = jnp.arange(own, dtype=jnp.int32)
    first = jnp.sum(own_needed[None, :] * (places[None, :] < places[:, None]), axis=1)
    goal = jnp.where(own_near > 0, rank + first[:, None] * GROUP, -1)
    capacity = own * CAPACITY
    slots = jnp.arange(capacity, dtype=jnp.int32)
    hit = goal.reshape(1, own * tiles) == slots[:, None]
    known = jnp.tile(ids + 1, own)[None]
    near_ids = (jnp.sum(jnp.where(hit, known, 0), axis=1) - 1).astype(jnp.int32)
    group_ids = jnp.arange(capacity // GROUP, dtype=jnp.int32)
    side = jnp.sum(group_ids[:, None] >= first[None, 1:], axis=1).astype(jnp.int32)

    near_ids, side, largest = lax.optimization_barrier((near_ids, side, largest))
    operands = (near_ids, side, points, padded, noise_var, right_side, start_guess)
    small = own * 4
    return tuple(
        lax.cond(
            largest <= small,
            functools.partial(solve, dims, small, 1),
            functools.partial(solve, dims, capacity // GROUP, 2),
            *operands,
        )
    )


def solution(mesh):
    placed = (
        P(("row", "col"), None, None),
        P(("row", "col"), None),
        P(("row", "col"), None, None),
        P(("row", "col"), None, None),
        P("row", "col", None, None),
    )
    return jax.shard_map(
        functools.partial(shards, (mesh.shape["row"], mesh.shape["col"])),
        mesh=mesh,
        in_specs=placed,
        out_specs=(P(("row", "col"), None, None), P(("row", "col"), None, None)),
        check_vma=False,
    )
```

profile of v0, /device:TPU:0, one launch (start us, length us, event | category | flops | bytes accessed | tf_op | source)
XLA Modules:
  0.0 79.0 jit_solution(17753346779281548308)
XLA Ops:
  0.6 0.7 copy.21
  1.3 13.8 %shard_map.69 = f32[32,2,8,256]{3,2,1,0:T(8,128)S(1)} custom-call(f32[2,8,256]{2,1,0:T(8,128)S(1)} %pad.4.refs_0_), custom_call_target="tpu_custom_call" | custom-call | tf_op jit(solution)/shard_map/pallas_call | solution.py:171
  15.1 0.3 fusion.9
  15.4 0.1 copy.22
  15.5 0.1 copy.23
  15.5 0.3 fusion
  15.8 0.1 convert_reduce_fusion
  15.9 0.1 dynamic_slice.7
  16.0 0.1 fusion.7
  16.2 0.1 multiply_reduce_fusion
  16.3 0.1 compare_select_fusion.1
  16.4 0.1 eq.15
  16.5 0.1 broadcast_in_dim.15
  16.5 0.1 select_reduce_fusion
  16.7 0.6 slice.3
  17.2 0.6 compare_convert_fusion
  17.9 0.0 copy-start
  17.9 0.1 reduce_sum.55
  18.0 0.1 fusion.5
  18.2 0.6 reduce_max.19
  19.5 58.2 %conditional.1 = ((f32[2,8,256]{2,1,0:T(8,128)S(1)}, f32[2,8,256]{2,1,0:T(8,128)S(1)})) conditional(s32[]{:T(128)} %convert_element_type.26, (s32[56]{0:T(128)S(1)}, s32[14]{0:T(128)S(1)}, f32[32,2,8,256]{3,2,1,0:T(8,128)S(1)}, f32[2,8,256]{2,1,0:T(8,128)S(1)}, f32[2,256]{1,0:T(2,128)S(1)}, /*index=5*/f32[2,8,256]{2,1,0:T(8,128)S(1)}, ...), branch_computations={%region_9.10_spmd, %region_10.11_spmd} | conditional | bytes 8 | solution.py:450
  19.7 58.0 %branch_1_fun.1 = (f32[2,8,256]{2,1,0:T(8,128)S(1)}, f32[2,8,256]{2,1,0:T(8,128)S(1)}) custom-call(s32[56]{0:T(128)S(1)} %get-tuple-element.35.near_ref, s32[14]{0:T(128)S(1)} %get-tuple-element.36.side_ref, f32[64,8,256]{2,1,0:T(8,128)S(1)} %bitcast.6, f32[2,8,256]{2,1,0:T(8,128)S(1)} %get-tuple-element.38.own_points_ref, ...), custom_call_target="tpu_custom_call" | custom-call | tf_op jit(solution)/shard_map/cond/branch_1_fun/pallas_call | solution.py:392
  77.7 0.6 copy.30
  78.3 0.6 copy.31
  (14 shorter events, 0.1 us)
Async XLA Ops:
  17.9 1.6 %copy-start = (f32[2,8,256]{2,1,0:T(8,128)S(1)}, f32[2,8,256]{2,1,0:T(8,128)}, u32[]{:S(2)}) copy-start(f32[2,8,256]{2,1,0:T(8,128)} %param.9) | copy-start | bytes 49156
  17.9 1.6 %copy-start.1 = (f32[2,8,256]{2,1,0:T(8,128)S(1)}, f32[2,8,256]{2,1,0:T(8,128)}, u32[]{:S(2)}) copy-start(f32[2,8,256]{2,1,0:T(8,128)} %param.10) | copy-start | bytes 49156
  18.8 0.7 copy-start.2
where the time goes:
time: 79.2 us; the launch traced here: 79 us
  Pallas kernels  71.8 us (91%)
  local copies, waits for them, and re-layouts  2.99 us (4%)
  other arithmetic  2.51 us (3%)
  between operations  1.43 us (2%)
    pallas_call x1, Pallas kernels, solve(): pl.pallas_call(functools.partial(solve_kernel, dims, groups), out_shape=[...  58 us
    pallas_call x1, Pallas kernels, all_gather(): pl.pallas_call(functools.partial(gather_kernel, dims), out_shape=jax.Shap...  13.8 us
    unnamed x9, local copies, waits for them, and re-layouts  1.92 us

commit v1 on v0

--- a/solution.py
+++ b/solution.py
@@ -96,35 +96,41 @@
     for k in reversed(range(1, zs)):
         for a in range(count):
             along_z[k, a] = send(a, ins[a], mine, device(x, flip(z, k, zs), y, c))
-    yield
-    for a in range(count):
-        local[a].wait()
-
     if xs == 2 and ys == 2:
         across_by = ((1 - x, 1 - y), ((x + c) % 2, (y + 1 - c) % 2), ((x + 1 - c) % 2, (y + c) % 2))
         arrivals, swaps = [], []
-        for k in range(zs):
+
+        def hand_on(k):
             level = flip(z, k, zs)
             for a in range(count):
                 if k:
                     along_z[k, a].wait_recv()
                 place = slot(x, level, y, c)
+                source = outs[a].at[place] if k else ins[a]
                 for xx, yy in across_by:
-                    copy = send(a, outs[a].at[place], place, device(xx, z, yy, c))
+                    copy = send(a, source, place, device(xx, z, yy, c))
                     arrivals.append((copy, a, slot(xx, level, yy, c)))
-                swaps.append(send(a, outs[a].at[place], place, other))
+                swaps.append(send(a, source, place, other))
+
+        hand_on(0)
         yield
-        for number, way in enumerate((1, 2, 0)):
+        for k in range(1, zs):
+            hand_on(k)
+        for way in (1, 2, 0):
             for copy, a, place in arrivals[way::3]:
                 copy.wait_recv()
                 swaps.append(send(a, outs[a].at[place], place, other))
-            if number == 1:
-                yield
         for copy in swaps:
             copy.wait_recv()
         for copy in sent:
             copy.wait_send()
+        for copy in local:
+            copy.wait()
         return
+
+    yield
+    for copy in local:
+        copy.wait()
 
     def across(places, targets):
         for place in places:
@@ -155,44 +161,45 @@
     settle()
 
 
-def gather_kernel(dims, *refs):
-    in_ref, out_ref, send_sem, recv_sem, local_sem = refs
+def gather_kernel(dims, count, *refs):
+    ins, outs = refs[:count], refs[count : 2 * count]
+    send_sem, recv_sem, local_sem = refs[2 * count :]
     partners = gather_partners(dims)
     barrier = pltpu.get_barrier_semaphore()
     for partner in partners:
         pl.semaphore_signal(barrier, inc=1, device_id=partner, device_id_type=MESH)
     pl.semaphore_wait(barrier, len(partners))
-    for _ in gather(dims, [in_ref], [out_ref], send_sem, recv_sem, local_sem):
+    for _ in gather(dims, ins, outs, send_sem, recv_sem, local_sem):
         pass
 
 
-def all_gather(dims, collective_id, slab):
+def all_gather(dims, collective_id, *slabs):
     devices = dims[0] * dims[1] * dims[2] * dims[3]
+    count = len(slabs)
     return pl.pallas_call(
-        functools.partial(gather_kernel, dims),
-        out_shape=jax.ShapeDtypeStruct((devices,) + slab.shape, slab.dtype),
-        in_specs=[VMEM_SPEC],
-        out_specs=VMEM_SPEC,
+        functools.partial(gather_kernel, dims, count),
+        out_shape=[jax.ShapeDtypeStruct((devices,) + slab.shape, slab.dtype) for slab in slabs],
+        in_specs=[VMEM_SPEC] * count,
+        out_specs=[VMEM_SPEC] * count,
         scratch_shapes=[
-            pltpu.SemaphoreType.DMA((devices - 1,)),
-            pltpu.SemaphoreType.DMA((devices - 1,)),
-            pltpu.SemaphoreType.DMA((1,)),
+            pltpu.SemaphoreType.DMA((count * (devices - 1),)),
+            pltpu.SemaphoreType.DMA((count * (devices - 1),)),
+            pltpu.SemaphoreType.DMA((count,)),
         ],
         compiler_params=pltpu.CompilerParams(collective_id=collective_id, has_side_effects=True),
-    )(slab)
+    )(*slabs)
 
 
 def split_rows(values):
-    high = values.astype(jnp.bfloat16)
-    low = (values - high.astype(jnp.float32)).astype(jnp.bfloat16)
-    return jnp.concatenate([high, low], axis=0)
+    rest = values - values.astype(jnp.bfloat16).astype(jnp.float32)
+    return jnp.concatenate([values, rest], axis=0).astype(jnp.bfloat16)
 
 
 def solve_kernel(
     dims, groups,
-    near_ref, side_ref, points_ref, own_points_ref, noise_ref, right_ref, guess_ref,
+    near_ref, side_ref, points_ref, own_points_ref, noise_ref, right_ref, guess_ref, guesses_ref,
     field_out, residual_out,
-    buffers, dir_ref, vectors_ref, blocks, outgoing, dot_ref, dots_ref,
+    buffer0, buffer1, buffer2, dir_ref, blocks, outgoing, dot_ref, dots_ref,
     send_sem, recv_sem, local_sem, dot_send, dot_recv,
 ):
     cols = dims[1] * dims[2] * dims[3]
@@ -215,13 +222,16 @@
 
     def spreading(number, source):
         return gather(
-            dims, [source], [buffers.at[number]],
+            dims, [source], [(buffer0, buffer1, buffer2)[number]],
             send_sem.at[number], recv_sem.at[number], local_sem.at[number],
         )
 
-    def spread(number, source):
-        for _ in spreading(number, source):
-            pass
+    def spread(number, shadow=None):
+        result = None
+        for _ in spreading(number, outgoing.at[number]):
+            if shadow is not None:
+                result, shadow = shadow(), None
+        return result
 
     rows = 32
     block = 2 * tile
@@ -251,11 +261,12 @@
             blocks[pl.ds(at, rows), :] = low
         return carry
 
-    def image_of():
+    def image_of(fetch):
         def step(g, totals):
             parts = []
             for i in range(GROUP):
-                part = vectors_ref[jnp.maximum(near_ref[g * GROUP + i], 0)]
+                near = jnp.maximum(near_ref[g * GROUP + i], 0)
+                part = split_rows(fetch(near // own, near % own))
                 parts += [part, part]
             first = pl.multiple_of(g * GROUP * block, GROUP * block)
             term = jnp.dot(
@@ -282,75 +293,76 @@
     zero = jnp.zeros((rhs, tile), jnp.float32)
     noise = [noise_ref[p : p + 1, :] for p in range(own)]
 
-    shares = 5
-    bounds = [groups * GROUP // 2 * i // shares * 2 for i in range(shares + 1)]
-    lax.fori_loop(bounds[0], bounds[1], build, 0, unroll=2)
+    def over_sums(body, count):
+        start = (zero,) * count
+        return [jnp.sum(total, axis=1, keepdims=True) for total in over_tiles(body, start)]
+
+    lax.fori_loop(0, groups * GROUP, build, 0, unroll=2)
     pl.semaphore_wait(barrier, devices - 1)
-    built = 1
-    for _ in spreading(0, guess_ref):
-        lax.fori_loop(bounds[built], bounds[built + 1], build, 0, unroll=2)
-        built += 1
-    lax.fori_loop(bounds[built], bounds[shares], build, 0, unroll=2)
-
-    def take_guess(i, p, carry):
-        vectors_ref[i * own + p] = split_rows(buffers[0, i, p])
-        return carry
-
-    over_tiles(take_guess, 0)
-    for p, image in enumerate(image_of()):
+
+    for p, image in enumerate(image_of(lambda i, p: guesses_ref[i, p])):
         outgoing[0, p] = right_ref[p] - (image + noise[p] * guess_ref[p])
-    spread(1, outgoing.at[0])
-
-    def take_residual(i, p, total):
-        value = buffers[1, i, p]
-        dir_ref[i, p] = value
-        vectors_ref[i * own + p] = split_rows(value)
-        return total + value * value
-
-    norm = jnp.sum(over_tiles(take_residual, zero), axis=1, keepdims=True)
-    for p in range(own):
-        field_out[p] = guess_ref[p]
-    for iteration in range(1, ITERS):
-        for p, image in enumerate(image_of()):
-            outgoing[iteration, p] = image + noise[p] * dir_ref[me, p]
-        spread(1 + iteration, outgoing.at[iteration])
-
-        def dots(i, p, total):
-            return total + dir_ref[i, p] * buffers[1 + iteration, i, p]
-
-        inner = jnp.sum(over_tiles(dots, zero), axis=1, keepdims=True)
-        step_size = norm / inner
-        for p in range(own):
-            field_out[p] = field_out[p] + step_size * dir_ref[me, p]
-
-        def descend(i, p, total):
-            value = buffers[1, i, p] - step_size * buffers[1 + iteration, i, p]
-            buffers[1, i, p] = value
-            return total + value * value
-
-        norm_next = jnp.sum(over_tiles(descend, zero), axis=1, keepdims=True)
-        turn = norm_next / norm
+    spread(0)
+
+    for p, image in enumerate(image_of(lambda i, p: buffer0[i, p])):
+        outgoing[1, p] = image + noise[p] * outgoing[0, p]
+
+    def norm_of_residual():
+        def square(i, p, totals):
+            value = buffer0[i, p]
+            return (totals[0] + value * value,)
+
+        return over_sums(square, 1)[0]
+
+    norm0 = spread(1, norm_of_residual)
+
+    for p, image in enumerate(image_of(lambda i, p: buffer1[i, p])):
+        outgoing[2, p] = image + noise[p] * outgoing[1, p]
+
+    def first_step():
+        def dots(i, p, totals):
+            return (totals[0] + buffer0[i, p] * buffer1[i, p],)
+
+        step0 = norm0 / over_sums(dots, 1)[0]
+
+        def descend(i, p, totals):
+            value = buffer0[i, p] - step0 * buffer1[i, p]
+            dir_ref[i, p] = value
+            return (totals[0] + value * value,)
+
+        norm1 = over_sums(descend, 1)[0]
+        turn0 = norm1 / norm0
 
         def redirect(i, p, carry):
-            value = buffers[1, i, p] + turn * dir_ref[i, p]
-            dir_ref[i, p] = value
-            vectors_ref[i * own + p] = split_rows(value)
+            value = dir_ref[i, p]
+            dir_ref[i, p] = value + turn0 * buffer0[i, p]
+            buffer0[i, p] = value
             return carry
 
         over_tiles(redirect, 0)
-        norm = norm_next
-
-    images, total = [], zero
-    for p, image in enumerate(image_of()):
-        value = dir_ref[me, p]
-        image = image + noise[p] * value
+        return step0, norm1, turn0
+
+    step0, norm1, turn0 = spread(2, first_step)
+    grow0 = 1.0 + turn0
+
+    def image1(i, p):
+        return grow0 * buffer1[i, p] - step0 * buffer2[i, p]
+
+    own_image1 = [grow0 * outgoing[1, p] - step0 * outgoing[2, p] for p in range(own)]
+    own_residual1 = [outgoing[0, p] - step0 * outgoing[1, p] for p in range(own)]
+    own_dir1 = [own_residual1[p] + turn0 * outgoing[0, p] for p in range(own)]
+    images, totals = [], [zero] * 3
+    for p, image in enumerate(image_of(image1)):
+        image = image + noise[p] * own_image1[p]
         images.append(image)
-        total = total + value * image
-    eye = lax.broadcasted_iota(jnp.int32, (rhs, 128), 0) == lax.broadcasted_iota(
-        jnp.int32, (rhs, 128), 1
-    )
-    share = jnp.sum(total, axis=1, keepdims=True)
-    row = jnp.sum(jnp.where(eye, share, 0.0), axis=0, keepdims=True)
+        values = (own_residual1[p], own_image1[p], own_dir1[p])
+        totals = [total + value * image for total, value in zip(totals, values)]
+    lanes = lax.broadcasted_iota(jnp.int32, (rhs, 128), 1)
+    eyes = [lanes == lax.broadcasted_iota(jnp.int32, (rhs, 128), 0) + n * rhs for n in range(3)]
+    row = jnp.zeros((1, 128), jnp.float32)
+    for eye, total in zip(eyes, totals):
+        share = jnp.sum(total, axis=1, keepdims=True)
+        row = row + jnp.sum(jnp.where(eye, share, 0.0), axis=0, keepdims=True)
     dot_ref[...] = row
     dots_ref[me] = row
 
@@ -373,31 +385,66 @@
         return carry
 
     lax.fori_loop(1, devices, start_dot, 0)
+
+    def second_dots(i, p, totals):
+        direction = dir_ref[i, p]
+        image = buffer1[i, p] - step0 * buffer2[i, p]
+        return (
+            totals[0] + direction * image1(i, p),
+            totals[1] + direction * image,
+        )
+
+    dir_image1, dir_image = over_sums(second_dots, 2)
+    step1 = norm1 / dir_image1
+
+    def second_descend(i, p, totals):
+        image = buffer1[i, p] - step0 * buffer2[i, p]
+        turned = image1(i, p)
+        value = buffer0[i, p] - step1 * turned
+        return (
+            totals[0] + value * value,
+            totals[1] + value * image,
+            totals[2] + value * turned,
+        )
+
+    norm2, next_image, next_image1 = over_sums(second_descend, 3)
+    turn1 = norm2 / norm1
+    known = next_image + turn1 * (next_image1 + dir_image + turn1 * dir_image1)
+    fields, residuals, directions, applied = [], [], [], []
+    for p in range(own):
+        residual = own_residual1[p] - step1 * own_image1[p]
+        fields.append(guess_ref[p] + step0 * outgoing[0, p] + step1 * own_dir1[p])
+        residuals.append(residual)
+        directions.append(residual + turn1 * own_dir1[p])
+        applied.append(
+            outgoing[1, p] - step0 * outgoing[2, p] - step1 * images[p] + turn1 * own_image1[p]
+        )
+
     lax.fori_loop(1, devices, wait_dot, 0)
-    inner = jnp.sum(dots_ref[...], axis=0)
-    inner = jnp.sum(jnp.where(eye, inner, 0.0), axis=1, keepdims=True)
-    step_size = norm / inner
+    sums = jnp.sum(dots_ref[...], axis=0)
+    first, second, third = [
+        jnp.sum(jnp.where(eye, sums, 0.0), axis=1, keepdims=True) for eye in eyes
+    ]
+    step2 = norm2 / (known - step1 * (first - step1 * second + turn1 * third))
     for p in range(own):
-        field_out[p] = field_out[p] + step_size * dir_ref[me, p]
-        residual_out[p] = buffers[1, me, p] - step_size * images[p]
+        field_out[p] = fields[p] + step2 * directions[p]
+        residual_out[p] = residuals[p] - step2 * applied[p]
 
 
 def solve(dims, groups, collective_id, *operands):
     devices = dims[0] * dims[1] * dims[2] * dims[3]
     points, right = operands[2], operands[5]
-    tiles, tile = points.shape[0], points.shape[2]
+    tile = points.shape[2]
     own, rhs, _ = right.shape
     dma = pltpu.SemaphoreType.DMA
-    phases = 1 + ITERS
+    phases = ITERS
     return pl.pallas_call(
         functools.partial(solve_kernel, dims, groups),
         out_shape=[jax.ShapeDtypeStruct(right.shape, jnp.float32)] * 2,
-        in_specs=[SMEM_SPEC] * 2 + [VMEM_SPEC] * 5,
+        in_specs=[SMEM_SPEC] * 2 + [VMEM_SPEC] * 6,
         out_specs=[VMEM_SPEC] * 2,
         scratch_shapes=[
-            pltpu.VMEM((phases, devices, own, rhs, tile), jnp.float32),
-            pltpu.VMEM((devices, own, rhs, tile), jnp.float32),
-            pltpu.VMEM((tiles, 2 * rhs, tile), jnp.bfloat16),
+            *[pltpu.VMEM((devices, own, rhs, tile), jnp.float32)] * (phases + 1),
             pltpu.VMEM((groups * GROUP * 2 * tile, tile), jnp.bfloat16),
             pltpu.VMEM((ITERS, own, rhs, tile), jnp.float32),
             pltpu.VMEM((1, 128), jnp.float32),
@@ -421,7 +468,8 @@
     tiles = own * devices
     me = lax.axis_index("row") * mesh_shape[1] + lax.axis_index("col")
     padded = jnp.pad(coords, ((0, 0), (0, 5), (0, 0)))
-    points = all_gather(dims, 0, padded).reshape(tiles, 8, tile)
+    points, guesses = all_gather(dims, 0, padded, start_guess)
+    points = points.reshape(tiles, 8, tile)
 
     low, high = jnp.min(points, axis=2), jnp.max(points, axis=2)
     gap = jnp.maximum(low[None] - high[:, None], low[:, None] - high[None])
@@ -444,7 +492,7 @@
     side = jnp.sum(group_ids[:, None] >= first[None, 1:], axis=1).astype(jnp.int32)
 
     near_ids, side, largest = lax.optimization_barrier((near_ids, side, largest))
-    operands = (near_ids, side, points, padded, noise_var, right_side, start_guess)
+    operands = (near_ids, side, points, padded, noise_var, right_side, start_guess, guesses)
     small = own * 4
     return tuple(
         lax.cond(

time: 79.2 us -> 72.2 us (0.912)
  Pallas kernels: 71.8 us -> 65 us
    pallas_call x1, Pallas kernels: 58 us -> 48.5 us  [solve(): pl.pallas_call(functools.partial(solve_kernel, dims, groups), out_shape=[...]
    pallas_call x1, Pallas kernels: 13.8 us -> 16.5 us  [all_gather(): pl.pallas_call(functools.partial(gather_kernel, dims, count), out_shape=[...]
where the time goes in v1:
time: 72.2 us; the launch traced here: 71.9 us
  Pallas kernels  65 us (90%)
  local copies, waits for them, and re-layouts  2.99 us (4%)
  other arithmetic  2.5 us (3%)
  between operations  1.42 us (2%)
    pallas_call x1, Pallas kernels, solve(): pl.pallas_call(functools.partial(solve_kernel, dims, groups), out_shape=[...  48.5 us
    pallas_call x1, Pallas kernels, all_gather(): pl.pallas_call(functools.partial(gather_kernel, dims, count), out_shape=[...  16.5 us
    unnamed x9, local copies, waits for them, and re-layouts  1.93 us

profile of v1, /device:TPU:0, one launch (start us, length us, event | category | flops | bytes accessed | tf_op | source)
XLA Modules:
  0.0 71.9 jit_solution(11793968970306128160)
XLA Ops:
  0.6 0.7 copy.15
  1.4 16.5 %shard_map.63 = (f32[32,2,8,256]{3,2,1,0:T(8,128)S(1)}, f32[32,2,8,256]{3,2,1,0:T(8,128)S(1)}) custom-call(f32[2,8,256]{2,1,0:T(8,128)S(1)} %pad.4.refs_0_, f32[2,8,256]{2,1,0:T(8,128)S(1)} %copy-done), custom_call_target="tpu_custom_call" | custom-call | tf_op jit(solution)/shard_map/pallas_call | solution.py:179
  17.8 0.3 fusion.9
  18.1 0.1 copy.16
  18.2 0.1 copy.17
  18.2 0.3 fusion
  18.5 0.1 convert_reduce_fusion
  18.6 0.1 dynamic_slice.7
  18.7 0.1 fusion.7
  18.9 0.1 multiply_reduce_fusion
  19.0 0.1 compare_select_fusion.1
  19.1 0.1 eq.15
  19.2 0.1 broadcast_in_dim.15
  19.2 0.1 select_reduce_fusion
  19.4 0.6 slice.3
  20.0 0.6 compare_convert_fusion
  20.6 0.1 reduce_sum.55
  20.7 0.0 copy-start.1
  20.7 0.1 fusion.5
  20.9 0.6 reduce_max.19
  22.2 48.5 %conditional.1 = ((f32[2,8,256]{2,1,0:T(8,128)S(1)}, f32[2,8,256]{2,1,0:T(8,128)S(1)})) conditional(s32[]{:T(128)} %convert_element_type.26, (s32[56]{0:T(128)S(1)}, s32[14]{0:T(128)S(1)}, f32[64,8,256]{2,1,0:T(8,128)S(1)}, f32[2,8,256]{2,1,0:T(8,128)S(1)}, f32[2,256]{1,0:T(2,128)S(1)}, /*index=5*/f32[2,8,256]{2,1,0:T(8,128)S(1)}, ...), branch_computations={%region_9.10_spmd, %region_10.11_spmd} | conditional | bytes 8 | solution.py:498
  22.2 48.5 %branch_1_fun.1 = (f32[2,8,256]{2,1,0:T(8,128)S(1)}, f32[2,8,256]{2,1,0:T(8,128)S(1)}) custom-call(s32[56]{0:T(128)S(1)} %get-tuple-element.40.near_ref, s32[14]{0:T(128)S(1)} %get-tuple-element.41.side_ref, f32[64,8,256]{2,1,0:T(8,128)S(1)} %get-tuple-element.42.points_ref, f32[2,8,256]{2,1,0:T(8,128)S(1)} %get-tuple-element.43.own_points_ref, ...), custom_call_target="tpu_custom_call" | custom-call | tf_op jit(solution)/shard_map/cond/branch_1_fun/pallas_call | solution.py:441
  70.7 0.6 copy.24
  71.3 0.6 copy.25
  (14 shorter events, 0.1 us)
Async XLA Ops:
  0.6 0.7 %copy-start = (f32[2,8,256]{2,1,0:T(8,128)S(1)}, f32[2,8,256]{2,1,0:T(8,128)}, u32[]{:S(2)}) copy-start(f32[2,8,256]{2,1,0:T(8,128)} %refs_1_.1) | copy-start | bytes 49156
  20.7 1.4 %copy-start.1 = (f32[2,8,256]{2,1,0:T(8,128)S(1)}, f32[2,8,256]{2,1,0:T(8,128)}, u32[]{:S(2)}) copy-start(f32[2,8,256]{2,1,0:T(8,128)} %param.9) | copy-start | bytes 49156
  21.5 0.7 copy-start.2

commit v2 on v1

--- a/solution.py
+++ b/solution.py
@@ -110,25 +110,29 @@
                 for xx, yy in across_by:
                     copy = send(a, source, place, device(xx, z, yy, c))
                     arrivals.append((copy, a, slot(xx, level, yy, c)))
-                swaps.append(send(a, source, place, other))
+                swaps.append((a, send(a, source, place, other)))
 
         hand_on(0)
-        yield
+        yield "sent"
         for k in range(1, zs):
             hand_on(k)
-        for way in (1, 2, 0):
-            for copy, a, place in arrivals[way::3]:
-                copy.wait_recv()
-                swaps.append(send(a, outs[a].at[place], place, other))
-        for copy in swaps:
-            copy.wait_recv()
+        for first in range(count):
+            for way in (1, 2, 0):
+                for copy, a, place in arrivals[way::3]:
+                    if a == first:
+                        copy.wait_recv()
+                        swaps.append((a, send(a, outs[a].at[place], place, other)))
+        for first in range(count):
+            for a, copy in swaps:
+                if a == first:
+                    copy.wait_recv()
+            local[first].wait()
+            if first == 0:
+                yield "whole"
         for copy in sent:
             copy.wait_send()
-        for copy in local:
-            copy.wait()
         return
 
-    yield
     for copy in local:
         copy.wait()
 
@@ -159,35 +163,112 @@
         [other],
     )
     settle()
-
-
-def gather_kernel(dims, count, *refs):
-    ins, outs = refs[:count], refs[count : 2 * count]
-    send_sem, recv_sem, local_sem = refs[2 * count :]
+    yield "whole"
+
+
+def column_of(matrix, lane):
+    lanes = lax.broadcasted_iota(jnp.int32, matrix.shape, 1)
+    return jnp.sum(jnp.where(lanes == lane, matrix, 0.0), axis=1, keepdims=True)
+
+
+def list_near(own, devices, me, points_ref, ids_ref, side_ref, largest_ref):
+    tiles = own * devices
+    table = jnp.concatenate([points_ref[:, 4 * p + 3, :128] for p in range(own)], axis=0)
+    across = table.T
+    far = None
+    for component in range(3):
+        low, high = table[:, component : component + 1], table[:, component + 3 : component + 4]
+        low_row, high_row = across[component : component + 1], across[component + 3 : component + 4]
+        gap = jnp.maximum(low - high_row, low_row - high)
+        far = gap if far is None else jnp.maximum(far, gap)
+    near = jnp.where(far < 1.0, 1.0, 0.0)
+    needed = jnp.ceil(jnp.sum(near, axis=1, keepdims=True) * (1.0 / GROUP))
+    groups = sum(needed[p * devices : (p + 1) * devices] for p in range(own))
+    largest_ref[0] = jnp.max(groups).astype(jnp.int32)
+
+    rows = lax.broadcasted_iota(jnp.int32, (tiles, tiles), 0)
+    earlier = rows > lax.broadcasted_iota(jnp.int32, (tiles, tiles), 1)
+    rank = jnp.dot(
+        jnp.where(earlier, 1.0, 0.0).astype(jnp.bfloat16),
+        near.astype(jnp.bfloat16),
+        preferred_element_type=jnp.float32,
+    )
+    slots = lax.broadcasted_iota(jnp.int32, (tiles, ids_ref.shape[1]), 1).astype(jnp.float32)
+    place = lax.broadcasted_iota(jnp.int32, (tiles, 1), 0)
+    tile_ids = (place % devices * own + place // devices + 1).astype(jnp.float32)
+    group_ids = lax.broadcasted_iota(jnp.int32, side_ref.shape, 1).astype(jnp.float32)
+    found, side = 0.0, jnp.zeros(side_ref.shape, jnp.float32)
+    first = jnp.zeros((1, 1), jnp.float32)
+    for p in range(own):
+        lane = p * devices + me
+        chosen = column_of(near, lane)
+        goal = jnp.where(chosen > 0.0, column_of(rank, lane) + first * GROUP, -1.0)
+        found = found + jnp.where(goal == slots, tile_ids, 0.0)
+        if p:
+            side = side + jnp.where(group_ids >= first, 1.0, 0.0)
+        first = first + jnp.ceil(jnp.sum(chosen, axis=0, keepdims=True) * (1.0 / GROUP))
+    ids_ref[...] = (jnp.sum(found, axis=0, keepdims=True) - 1.0).astype(jnp.int32)
+    side_ref[...] = side.astype(jnp.int32)
+
+
+def gather_kernel(dims, coords_ref, guess_ref, points_ref, guesses_ref, ids_ref, side_ref,
+                  largest_ref, slab_ref, send_sem, recv_sem, local_sem):
+    own = coords_ref.shape[1]
+    cols = dims[1] * dims[2] * dims[3]
+    devices = dims[0] * cols
     partners = gather_partners(dims)
     barrier = pltpu.get_barrier_semaphore()
     for partner in partners:
         pl.semaphore_signal(barrier, inc=1, device_id=partner, device_id_type=MESH)
+    lanes = lax.broadcasted_iota(jnp.int32, (1, coords_ref.shape[2]), 1)
+    for p in range(own):
+        box = jnp.zeros(lanes.shape, jnp.float32)
+        for component in range(3):
+            row = coords_ref[component, p : p + 1, :]
+            slab_ref[4 * p + component : 4 * p + component + 1, :] = row
+            box = jnp.where(lanes == component, jnp.min(row, axis=1, keepdims=True), box)
+            box = jnp.where(lanes == component + 3, jnp.max(row, axis=1, keepdims=True), box)
+        slab_ref[4 * p + 3 : 4 * p + 4, :] = box
     pl.semaphore_wait(barrier, len(partners))
-    for _ in gather(dims, ins, outs, send_sem, recv_sem, local_sem):
-        pass
-
-
-def all_gather(dims, collective_id, *slabs):
+    ins, outs = [slab_ref, guess_ref], [points_ref, guesses_ref]
+    me = lax.axis_index("row") * cols + lax.axis_index("col")
+    for stage in gather(dims, ins, outs, send_sem, recv_sem, local_sem):
+        if stage == "whole":
+            list_near(own, devices, me, points_ref, ids_ref, side_ref, largest_ref)
+
+
+def all_gather(dims, collective_id, coords, guess):
     devices = dims[0] * dims[1] * dims[2] * dims[3]
-    count = len(slabs)
+    _, own, tile = coords.shape
+    wide = -(-own * CAPACITY // 128) * 128
     return pl.pallas_call(
-        functools.partial(gather_kernel, dims, count),
-        out_shape=[jax.ShapeDtypeStruct((devices,) + slab.shape, slab.dtype) for slab in slabs],
-        in_specs=[VMEM_SPEC] * count,
-        out_specs=[VMEM_SPEC] * count,
+        functools.partial(gather_kernel, dims),
+        out_shape=[
+            jax.ShapeDtypeStruct((devices, 4 * own, tile), jnp.float32),
+            jax.ShapeDtypeStruct((devices,) + guess.shape, jnp.float32),
+            jax.ShapeDtypeStruct((1, wide), jnp.int32),
+            jax.ShapeDtypeStruct((1, wide), jnp.int32),
+            jax.ShapeDtypeStruct((1,), jnp.int32),
+        ],
+        in_specs=[VMEM_SPEC] * 2,
+        out_specs=[VMEM_SPEC] * 4 + [SMEM_SPEC],
         scratch_shapes=[
-            pltpu.SemaphoreType.DMA((count * (devices - 1),)),
-            pltpu.SemaphoreType.DMA((count * (devices - 1),)),
-            pltpu.SemaphoreType.DMA((count,)),
+            pltpu.VMEM((4 * own, tile), jnp.float32),
+            pltpu.SemaphoreType.DMA((2 * (devices - 1),)),
+            pltpu.SemaphoreType.DMA((2 * (devices - 1),)),
+            pltpu.SemaphoreType.DMA((2,)),
         ],
         compiler_params=pltpu.CompilerParams(collective_id=collective_id, has_side_effects=True),
-    )(*slabs)
+    )(coords, guess)
+
+
+def three_parts(value):
+    parts = []
+    for _ in range(3):
+        part = value.astype(jnp.bfloat16).astype(jnp.float32)
+        parts.append(part)
+        value = value - part
+    return parts
 
 
 def split_rows(values):
@@ -197,15 +278,15 @@
 
 def solve_kernel(
     dims, groups,
-    near_ref, side_ref, points_ref, own_points_ref, noise_ref, right_ref, guess_ref, guesses_ref,
+    near_ref, side_ref, points_ref, noise_ref, right_ref, guess_ref, guesses_ref,
     field_out, residual_out,
-    buffer0, buffer1, buffer2, dir_ref, blocks, outgoing, dot_ref, dots_ref,
+    buffer0, buffer1, buffer2, dir_ref, blocks, own_side, centers, outgoing, dot_ref, dots_ref,
     send_sem, recv_sem, local_sem, dot_send, dot_recv,
 ):
     cols = dims[1] * dims[2] * dims[3]
     devices = dims[0] * cols
-    tiles, tile = points_ref.shape[0], points_ref.shape[2]
-    own, rhs, _ = right_ref.shape
+    own, rhs, tile = right_ref.shape
+    tiles = own * devices
     me = lax.axis_index("row") * cols + lax.axis_index("col")
 
     def peer(k):
@@ -228,31 +309,50 @@
 
     def spread(number, shadow=None):
         result = None
-        for _ in spreading(number, outgoing.at[number]):
-            if shadow is not None:
+        for stage in spreading(number, outgoing.at[number]):
+            if shadow is not None and result is None:
                 result, shadow = shadow(), None
         return result
 
     rows = 32
     block = 2 * tile
+    line = lax.broadcasted_iota(jnp.int32, (8, tile), 0)
+    blank = jnp.zeros((4, tile), jnp.float32)
+
+    def place_points(device, p):
+        slab = points_ref[device]
+        points = slab[:4]
+        for other in range(1, own):
+            points = jnp.where(p == other, slab[4 * other : 4 * other + 4], points)
+        return jnp.concatenate([points, blank], axis=0)
+
+    for p in range(own):
+        points = place_points(me, p)
+        center = jnp.floor(jnp.min(points, axis=1, keepdims=True))
+        points = jnp.where(line < 3, points - center, 0.0)
+        squares = jnp.sum(points * points, axis=0, keepdims=True)
+        value = jnp.where(line == 3, 16.0, jnp.where(line == 4, 16.0 * squares, -32.0 * points))
+        one, two, three = three_parts(value)
+        own_side[p] = jnp.concatenate([one, two, one, three, one, two], axis=0).astype(jnp.bfloat16)
+        centers[p] = jnp.broadcast_to(center, (8, tile))
 
     def build(e, carry):
-        left = points_ref[jnp.maximum(near_ref[e], 0)].T
-        right = own_points_ref[side_ref[e // GROUP]]
-        reach = jnp.minimum(near_ref[e] + 1, 1).astype(jnp.float32)
+        near = jnp.maximum(near_ref[0, e], 0)
+        p = side_ref[0, e // GROUP]
+        reach = jnp.minimum(near_ref[0, e] + 1, 1).astype(jnp.float32) * 4.0
+        points = jnp.where(line < 3, place_points(near // own, near % own) - centers[p], 0.0)
+        squares = jnp.sum(points * points, axis=0, keepdims=True)
+        value = jnp.where(line == 3, squares, jnp.where(line == 4, 1.0, points))
+        one, two, three = three_parts(value)
+        left = jnp.concatenate([one, one, two, one, three, two], axis=0).astype(jnp.bfloat16)
+        squared = lax.dot_general(
+            left, own_side[p], (((0,), (0,)), ((), ())), preferred_element_type=jnp.float32
+        )
         for chunk in range(tile // rows):
-            squared = None
-            for component in range(3):
-                spacing = (
-                    left[chunk * rows : (chunk + 1) * rows, component : component + 1]
-                    - right[component : component + 1, :]
-                )
-                term = spacing * spacing
-                squared = term if squared is None else squared + term
-            distance = squared * lax.rsqrt(jnp.maximum(squared, 1e-30))
-            remain = jnp.maximum(reach - distance, 0.0)
-            remain = remain * remain
-            weights = remain * remain * (4.0 * distance + 1.0)
+            spacing = jnp.maximum(squared[chunk * rows : (chunk + 1) * rows], 1e-30)
+            remain = jnp.maximum(reach - spacing * lax.rsqrt(spacing), 0.0)
+            twice = remain * remain
+            weights = twice * twice * (5.0 - remain)
             high = weights.astype(jnp.bfloat16)
             low = (weights - high.astype(jnp.float32)).astype(jnp.bfloat16)
             at = pl.multiple_of(e * block + chunk * rows, rows)
@@ -265,7 +365,7 @@
         def step(g, totals):
             parts = []
             for i in range(GROUP):
-                near = jnp.maximum(near_ref[g * GROUP + i], 0)
+                near = jnp.maximum(near_ref[0, g * GROUP + i], 0)
                 part = split_rows(fetch(near // own, near % own))
                 parts += [part, part]
             first = pl.multiple_of(g * GROUP * block, GROUP * block)
@@ -274,7 +374,7 @@
                 blocks[pl.ds(first, GROUP * block), :],
                 preferred_element_type=jnp.float32,
             )
-            place = side_ref[g].astype(jnp.float32)
+            place = side_ref[0, g].astype(jnp.float32)
             return tuple(
                 total + term * jnp.maximum(1.0 - jnp.abs(place - float(p)), 0.0)
                 for p, total in enumerate(totals)
@@ -282,7 +382,7 @@
 
         start = tuple(jnp.zeros((2 * rhs, tile), jnp.float32) for _ in range(own))
         totals = lax.fori_loop(0, groups, step, start, unroll=4 if groups % 4 == 0 else 2)
-        return [total[:rhs] + total[rhs:] for total in totals]
+        return [(total[:rhs] + total[rhs:]) * (1.0 / 256.0) for total in totals]
 
     def over_tiles(body, start):
         def one(i, carry):
@@ -433,19 +533,20 @@
 
 def solve(dims, groups, collective_id, *operands):
     devices = dims[0] * dims[1] * dims[2] * dims[3]
-    points, right = operands[2], operands[5]
-    tile = points.shape[2]
-    own, rhs, _ = right.shape
+    right = operands[4]
+    own, rhs, tile = right.shape
     dma = pltpu.SemaphoreType.DMA
     phases = ITERS
     return pl.pallas_call(
         functools.partial(solve_kernel, dims, groups),
         out_shape=[jax.ShapeDtypeStruct(right.shape, jnp.float32)] * 2,
-        in_specs=[SMEM_SPEC] * 2 + [VMEM_SPEC] * 6,
+        in_specs=[SMEM_SPEC] * 2 + [VMEM_SPEC] * 5,
         out_specs=[VMEM_SPEC] * 2,
         scratch_shapes=[
             *[pltpu.VMEM((devices, own, rhs, tile), jnp.float32)] * (phases + 1),
             pltpu.VMEM((groups * GROUP * 2 * tile, tile), jnp.bfloat16),
+            pltpu.VMEM((own, 48, tile), jnp.bfloat16),
+            pltpu.VMEM((own, 8, tile), jnp.float32),
             pltpu.VMEM((ITERS, own, rhs, tile), jnp.float32),
             pltpu.VMEM((1, 128), jnp.float32),
             pltpu.VMEM((devices, 1, 128), jnp.float32),
@@ -463,42 +564,16 @@
 
 def shards(mesh_shape, coords, noise_var, right_side, start_guess, tile_pairs):
     dims = factors(mesh_shape)
-    devices = mesh_shape[0] * mesh_shape[1]
-    own, _, tile = coords.shape
-    tiles = own * devices
-    me = lax.axis_index("row") * mesh_shape[1] + lax.axis_index("col")
-    padded = jnp.pad(coords, ((0, 0), (0, 5), (0, 0)))
-    points, guesses = all_gather(dims, 0, padded, start_guess)
-    points = points.reshape(tiles, 8, tile)
-
-    low, high = jnp.min(points, axis=2), jnp.max(points, axis=2)
-    gap = jnp.maximum(low[None] - high[:, None], low[:, None] - high[None])
-    near = jnp.all(gap < 1.0, axis=2).astype(jnp.int32)
-    needed = -(-jnp.sum(near, axis=1) // GROUP)
-    largest = jnp.max(jnp.sum(needed.reshape(devices, own), axis=1))
-    own_near = lax.dynamic_slice_in_dim(near, me * own, own)
-    own_needed = lax.dynamic_slice_in_dim(needed, me * own, own)
-    ids = jnp.arange(tiles, dtype=jnp.int32)
-    rank = jnp.sum(own_near[:, None, :] * (ids[None, None, :] < ids[None, :, None]), axis=2)
-    places = jnp.arange(own, dtype=jnp.int32)
-    first = jnp.sum(own_needed[None, :] * (places[None, :] < places[:, None]), axis=1)
-    goal = jnp.where(own_near > 0, rank + first[:, None] * GROUP, -1)
-    capacity = own * CAPACITY
-    slots = jnp.arange(capacity, dtype=jnp.int32)
-    hit = goal.reshape(1, own * tiles) == slots[:, None]
-    known = jnp.tile(ids + 1, own)[None]
-    near_ids = (jnp.sum(jnp.where(hit, known, 0), axis=1) - 1).astype(jnp.int32)
-    group_ids = jnp.arange(capacity // GROUP, dtype=jnp.int32)
-    side = jnp.sum(group_ids[:, None] >= first[None, 1:], axis=1).astype(jnp.int32)
-
-    near_ids, side, largest = lax.optimization_barrier((near_ids, side, largest))
-    operands = (near_ids, side, points, padded, noise_var, right_side, start_guess, guesses)
+    own = coords.shape[0]
+    placed = jnp.transpose(coords, (1, 0, 2))
+    points, guesses, near_ids, side, largest = all_gather(dims, 0, placed, start_guess)
+    operands = (near_ids, side, points, noise_var, right_side, start_guess, guesses)
     small = own * 4
     return tuple(
         lax.cond(
-            largest <= small,
+            largest[0] <= small,
             functools.partial(solve, dims, small, 1),
-            functools.partial(solve, dims, capacity // GROUP, 2),
+            functools.partial(solve, dims, own * CAPACITY // GROUP, 2),
             *operands,
         )
     )

time: 72.2 us -> 66.4 us (0.920)
  other arithmetic: 2.5 us -> 0 us
  Pallas kernels: 65 us -> 63 us
  local copies, waits for them, and re-layouts: 2.99 us -> 1.88 us
    pallas_call x1, Pallas kernels: 48.5 us -> 46.8 us  [solve(): pl.pallas_call(functools.partial(solve_kernel, dims, groups), out_shape=[...]
    unnamed x9 -> x8, local copies, waits for them, and re-layouts: 1.93 us -> 1.88 us
where the time goes in v2:
time: 66.4 us; the launch traced here: 66.1 us
  Pallas kernels  63 us (95%)
  local copies, waits for them, and re-layouts  1.88 us (3%)
  between operations  1.25 us (2%)
    pallas_call x1, Pallas kernels, solve(): pl.pallas_call(functools.partial(solve_kernel, dims, groups), out_shape=[...  46.8 us
    pallas_call x1, Pallas kernels, all_gather(): pl.pallas_call(functools.partial(gather_kernel, dims), out_shape=[jax.Sha...  16.2 us
    unnamed x8, local copies, waits for them, and re-layouts  1.88 us

profile of v2, /device:TPU:0, one launch (start us, length us, event | category | flops | bytes accessed | tf_op | source)
XLA Modules:
  0.0 66.1 jit_solution(5341388781774229233)
XLA Ops:
  0.6 0.0 copy-start
  0.6 0.0 copy-start.1
  0.6 16.2 %shard_map.63 = (f32[32,8,256]{2,1,0:T(8,128)S(1)}, f32[32,2,8,256]{3,2,1,0:T(8,128)S(1)}, s32[1,128]{1,0:T(1,128)S(1)}, s32[1,128]{1,0:T(1,128)S(1)}, s32[1]{0:T(128)}) custom-call(f32[3,2,256]{2,1,0:T(2,128)} %bitcast.2, f32[2,8,256]{2,1,0:T(8,128)} %guess_ref.1), custom_call_target="tpu_custom_call" | custom-call | tf_op jit(solution)/shard_map/pallas_call | solution.py:244
  17.4 0.0 copy-start.2
  17.4 0.0 copy-done
  17.4 0.0 copy-done.1
  17.4 0.7 copy-done.2
  18.1 46.8 %conditional.1 = ((f32[2,8,256]{2,1,0:T(8,128)S(1)}, f32[2,8,256]{2,1,0:T(8,128)S(1)})) conditional(s32[]{:T(128)} %bitcast.1, (s32[1,128]{1,0:T(1,128)S(1)}, s32[1,128]{1,0:T(1,128)S(1)}, f32[32,8,256]{2,1,0:T(8,128)S(1)}, f32[2,256]{1,0:T(2,128)S(1)}, f32[2,8,256]{2,1,0:T(8,128)S(1)}, /*index=5*/f32[2,8,256]{2,1,0:T(8,128)S(1)}, ...), branch_computations={%region_0.0_spmd, %region_1.0_spmd} | conditional | bytes 8 | solution.py:573
  18.1 46.8 %branch_1_fun.1 = (f32[2,8,256]{2,1,0:T(8,128)S(1)}, f32[2,8,256]{2,1,0:T(8,128)S(1)}) custom-call(s32[1,128]{1,0:T(1,128)S(1)} %get-tuple-element.35.near_ref, s32[1,128]{1,0:T(1,128)S(1)} %get-tuple-element.36.side_ref, f32[32,8,256]{2,1,0:T(8,128)S(1)} %get-tuple-element.37.points_ref, f32[2,256]{1,0:T(2,128)S(1)} %get-tuple-element.38.noise_ref, ...), custom_call_target="tpu_custom_call" | custom-call | tf_op jit(solution)/shard_map/cond/branch_1_fun/pallas_call | solution.py:540
  64.9 0.6 copy.16
  65.5 0.6 copy.17
Async XLA Ops:
  0.6 16.8 %copy-start = (f32[2,8,256]{2,1,0:T(8,128)S(1)}, f32[2,8,256]{2,1,0:T(8,128)}, u32[]{:S(2)}) copy-start(f32[2,8,256]{2,1,0:T(8,128)} %guess_ref.1) | copy-start | bytes 49156
  0.6 16.8 %copy-start.1 = (f32[2,8,256]{2,1,0:T(8,128)S(1)}, f32[2,8,256]{2,1,0:T(8,128)}, u32[]{:S(2)}) copy-start(f32[2,8,256]{2,1,0:T(8,128)} %param.9) | copy-start | bytes 49156
  17.4 0.7 %copy-start.2 = (f32[2,256]{1,0:T(2,128)S(1)}, f32[2,256]{1,0:T(2,128)}, u32[]{:S(2)}) copy-start(f32[2,256]{1,0:T(2,128)} %param.8) | copy-start | bytes 6148

commit v3 on v2

--- a/solution.py
+++ b/solution.py
@@ -50,6 +50,8 @@
     partners = [(x, (((z + k) % zs) * ys + y) * cs + c) for k in range(1, zs)]
     if xs == 2 and ys == 2:
         partners += [(1 - x, (z * ys + 1 - y) * cs + c)]
+        partners += [(1 - x, (z * ys + yy) * cs + 1 - c) for yy in range(ys)]
+        partners += [(x, (z * ys + 1 - y) * cs + 1 - c)]
     partners += [(x, (z * ys + (y + k) % ys) * cs + c) for k in range(1, ys)]
     partners += [((x + k) % xs, (z * ys + y) * cs + c) for k in range(1, xs)]
     partners += [(x, (z * ys + y) * cs + 1 - c)]
@@ -109,7 +111,9 @@
                 source = outs[a].at[place] if k else ins[a]
                 for xx, yy in across_by:
                     copy = send(a, source, place, device(xx, z, yy, c))
-                    arrivals.append((copy, a, slot(xx, level, yy, c)))
+                    arrivals.append((copy, a, k, slot(xx, level, yy, c)))
+                    if k == zs - 1:
+                        swaps.append((a, send(a, source, place, device(xx, z, yy, 1 - c))))
                 swaps.append((a, send(a, source, place, other)))
 
         hand_on(0)
@@ -118,10 +122,13 @@
             hand_on(k)
         for first in range(count):
             for way in (1, 2, 0):
-                for copy, a, place in arrivals[way::3]:
-                    if a == first:
+                for copy, a, k, place in arrivals[way::3]:
+                    if a == first and k < zs - 1:
                         copy.wait_recv()
                         swaps.append((a, send(a, outs[a].at[place], place, other)))
+            for copy, a, k, place in arrivals:
+                if a == first and k == zs - 1:
+                    copy.wait_recv()
         for first in range(count):
             for a, copy in swaps:
                 if a == first:
@@ -211,15 +218,24 @@
     side_ref[...] = side.astype(jnp.int32)
 
 
-def gather_kernel(dims, coords_ref, guess_ref, points_ref, guesses_ref, ids_ref, side_ref,
-                  largest_ref, slab_ref, send_sem, recv_sem, local_sem):
+def gather_kernel(dims, coords_in, guess_in, noise_in, points_ref, guesses_ref, noise_out, ids_ref, side_ref,
+                  largest_ref, coords_ref, guess_ref, slab_ref, send_sem, recv_sem,
+                  local_sem, fetch_sem):
     own = coords_ref.shape[1]
     cols = dims[1] * dims[2] * dims[3]
     devices = dims[0] * cols
+    fetches = [
+        pltpu.make_async_copy(coords_in, coords_ref, fetch_sem.at[0]),
+        pltpu.make_async_copy(guess_in, guess_ref, fetch_sem.at[1]),
+        pltpu.make_async_copy(noise_in, noise_out, fetch_sem.at[2]),
+    ]
+    for fetch in fetches:
+        fetch.start()
     partners = gather_partners(dims)
     barrier = pltpu.get_barrier_semaphore()
     for partner in partners:
         pl.semaphore_signal(barrier, inc=1, device_id=partner, device_id_type=MESH)
+    fetches[0].wait()
     lanes = lax.broadcasted_iota(jnp.int32, (1, coords_ref.shape[2]), 1)
     for p in range(own):
         box = jnp.zeros(lanes.shape, jnp.float32)
@@ -229,15 +245,17 @@
             box = jnp.where(lanes == component, jnp.min(row, axis=1, keepdims=True), box)
             box = jnp.where(lanes == component + 3, jnp.max(row, axis=1, keepdims=True), box)
         slab_ref[4 * p + 3 : 4 * p + 4, :] = box
+    fetches[1].wait()
     pl.semaphore_wait(barrier, len(partners))
     ins, outs = [slab_ref, guess_ref], [points_ref, guesses_ref]
     me = lax.axis_index("row") * cols + lax.axis_index("col")
     for stage in gather(dims, ins, outs, send_sem, recv_sem, local_sem):
         if stage == "whole":
             list_near(own, devices, me, points_ref, ids_ref, side_ref, largest_ref)
-
-
-def all_gather(dims, collective_id, coords, guess):
+    fetches[2].wait()
+
+
+def all_gather(dims, collective_id, coords, guess, noise):
     devices = dims[0] * dims[1] * dims[2] * dims[3]
     _, own, tile = coords.shape
     wide = -(-own * CAPACITY // 128) * 128
@@ -246,20 +264,24 @@
         out_shape=[
             jax.ShapeDtypeStruct((devices, 4 * own, tile), jnp.float32),
             jax.ShapeDtypeStruct((devices,) + guess.shape, jnp.float32),
+            jax.ShapeDtypeStruct(noise.shape, jnp.float32),
             jax.ShapeDtypeStruct((1, wide), jnp.int32),
             jax.ShapeDtypeStruct((1, wide), jnp.int32),
             jax.ShapeDtypeStruct((1,), jnp.int32),
         ],
-        in_specs=[VMEM_SPEC] * 2,
-        out_specs=[VMEM_SPEC] * 4 + [SMEM_SPEC],
+        in_specs=[ANY_SPEC] * 3,
+        out_specs=[VMEM_SPEC] * 5 + [SMEM_SPEC],
         scratch_shapes=[
+            pltpu.VMEM(coords.shape, jnp.float32),
+            pltpu.VMEM(guess.shape, jnp.float32),
             pltpu.VMEM((4 * own, tile), jnp.float32),
             pltpu.SemaphoreType.DMA((2 * (devices - 1),)),
             pltpu.SemaphoreType.DMA((2 * (devices - 1),)),
             pltpu.SemaphoreType.DMA((2,)),
+            pltpu.SemaphoreType.DMA((3,)),
         ],
         compiler_params=pltpu.CompilerParams(collective_id=collective_id, has_side_effects=True),
-    )(coords, guess)
+    )(coords, guess, noise)
 
 
 def three_parts(value):
@@ -279,8 +301,8 @@
 def solve_kernel(
     dims, groups,
     near_ref, side_ref, points_ref, noise_ref, right_ref, guess_ref, guesses_ref,
-    field_out, residual_out,
-    buffer0, buffer1, buffer2, dir_ref, blocks, own_side, centers, outgoing, dot_ref, dots_ref,
+    field_out, dir_out, residual_out, image_out, step_out,
+    buffer0, buffer1, buffer2, dir_ref, blocks, own_side, centers, squared0, squared1, outgoing, dot_ref, dots_ref,
     send_sem, recv_sem, local_sem, dot_send, dot_recv,
 ):
     cols = dims[1] * dims[2] * dims[3]
@@ -314,7 +336,7 @@
                 result, shadow = shadow(), None
         return result
 
-    rows = 32
+    rows = 16
     block = 2 * tile
     line = lax.broadcasted_iota(jnp.int32, (8, tile), 0)
     blank = jnp.zeros((4, tile), jnp.float32)
@@ -336,20 +358,22 @@
         own_side[p] = jnp.concatenate([one, two, one, three, one, two], axis=0).astype(jnp.bfloat16)
         centers[p] = jnp.broadcast_to(center, (8, tile))
 
-    def build(e, carry):
+    def measure(e, target):
         near = jnp.maximum(near_ref[0, e], 0)
         p = side_ref[0, e // GROUP]
-        reach = jnp.minimum(near_ref[0, e] + 1, 1).astype(jnp.float32) * 4.0
         points = jnp.where(line < 3, place_points(near // own, near % own) - centers[p], 0.0)
         squares = jnp.sum(points * points, axis=0, keepdims=True)
         value = jnp.where(line == 3, squares, jnp.where(line == 4, 1.0, points))
         one, two, three = three_parts(value)
         left = jnp.concatenate([one, one, two, one, three, two], axis=0).astype(jnp.bfloat16)
-        squared = lax.dot_general(
+        target[...] = lax.dot_general(
             left, own_side[p], (((0,), (0,)), ((), ())), preferred_element_type=jnp.float32
         )
+
+    def weigh(e, source):
+        reach = jnp.minimum(near_ref[0, e] + 1, 1).astype(jnp.float32) * 4.0
         for chunk in range(tile // rows):
-            spacing = jnp.maximum(squared[chunk * rows : (chunk + 1) * rows], 1e-30)
+            spacing = jnp.maximum(source[chunk * rows : (chunk + 1) * rows], 1e-30)
             remain = jnp.maximum(reach - spacing * lax.rsqrt(spacing), 0.0)
             twice = remain * remain
             weights = twice * twice * (5.0 - remain)
@@ -359,6 +383,12 @@
             blocks[pl.ds(at, rows), :] = high
             at = pl.multiple_of(e * block + tile + chunk * rows, rows)
             blocks[pl.ds(at, rows), :] = low
+
+    def build(pair, carry):
+        weigh(2 * pair, squared0)
+        measure(2 * pair + 1, squared1)
+        weigh(2 * pair + 1, squared1)
+        measure(jnp.minimum(2 * pair + 2, groups * GROUP - 1), squared0)
         return carry
 
     def image_of(fetch):
@@ -391,13 +421,14 @@
         return lax.fori_loop(0, tiles, one, start, unroll=16)
 
     zero = jnp.zeros((rhs, tile), jnp.float32)
-    noise = [noise_ref[p : p + 1, :] for p in range(own)]
 
     def over_sums(body, count):
         start = (zero,) * count
         return [jnp.sum(total, axis=1, keepdims=True) for total in over_tiles(body, start)]
 
-    lax.fori_loop(0, groups * GROUP, build, 0, unroll=2)
+    measure(0, squared0)
+    lax.fori_loop(0, groups * GROUP // 2, build, 0, unroll=4)
+    noise = [noise_ref[p : p + 1, :] for p in range(own)]
     pl.semaphore_wait(barrier, devices - 1)
 
     for p, image in enumerate(image_of(lambda i, p: guesses_ref[i, p])):
@@ -510,13 +541,12 @@
     norm2, next_image, next_image1 = over_sums(second_descend, 3)
     turn1 = norm2 / norm1
     known = next_image + turn1 * (next_image1 + dir_image + turn1 * dir_image1)
-    fields, residuals, directions, applied = [], [], [], []
     for p in range(own):
         residual = own_residual1[p] - step1 * own_image1[p]
-        fields.append(guess_ref[p] + step0 * outgoing[0, p] + step1 * own_dir1[p])
-        residuals.append(residual)
-        directions.append(residual + turn1 * own_dir1[p])
-        applied.append(
+        field_out[p] = guess_ref[p] + step0 * outgoing[0, p] + step1 * own_dir1[p]
+        residual_out[p] = residual
+        dir_out[p] = residual + turn1 * own_dir1[p]
+        image_out[p] = (
             outgoing[1, p] - step0 * outgoing[2, p] - step1 * images[p] + turn1 * own_image1[p]
         )
 
@@ -526,9 +556,7 @@
         jnp.sum(jnp.where(eye, sums, 0.0), axis=1, keepdims=True) for eye in eyes
     ]
     step2 = norm2 / (known - step1 * (first - step1 * second + turn1 * third))
-    for p in range(own):
-        field_out[p] = fields[p] + step2 * directions[p]
-        residual_out[p] = residuals[p] - step2 * applied[p]
+    step_out[...] = jnp.broadcast_to(step2, (rhs, tile))
 
 
 def solve(dims, groups, collective_id, *operands):
@@ -539,14 +567,16 @@
     phases = ITERS
     return pl.pallas_call(
         functools.partial(solve_kernel, dims, groups),
-        out_shape=[jax.ShapeDtypeStruct(right.shape, jnp.float32)] * 2,
+        out_shape=[jax.ShapeDtypeStruct(right.shape, jnp.float32)] * 4
+        + [jax.ShapeDtypeStruct((rhs, tile), jnp.float32)],
         in_specs=[SMEM_SPEC] * 2 + [VMEM_SPEC] * 5,
-        out_specs=[VMEM_SPEC] * 2,
+        out_specs=[VMEM_SPEC] * 5,
         scratch_shapes=[
             *[pltpu.VMEM((devices, own, rhs, tile), jnp.float32)] * (phases + 1),
             pltpu.VMEM((groups * GROUP * 2 * tile, tile), jnp.bfloat16),
             pltpu.VMEM((own, 48, tile), jnp.bfloat16),
             pltpu.VMEM((own, 8, tile), jnp.float32),
+            *[pltpu.VMEM((tile, tile), jnp.float32)] * 2,
             pltpu.VMEM((ITERS, own, rhs, tile), jnp.float32),
             pltpu.VMEM((1, 128), jnp.float32),
             pltpu.VMEM((devices, 1, 128), jnp.float32),
@@ -566,17 +596,17 @@
     dims = factors(mesh_shape)
     own = coords.shape[0]
     placed = jnp.transpose(coords, (1, 0, 2))
-    points, guesses, near_ids, side, largest = all_gather(dims, 0, placed, start_guess)
-    operands = (near_ids, side, points, noise_var, right_side, start_guess, guesses)
+    gathered = all_gather(dims, 0, placed, start_guess, noise_var)
+    points, guesses, noise, near_ids, side, largest = gathered
+    operands = (near_ids, side, points, noise, right_side, start_guess, guesses)
     small = own * 4
-    return tuple(
-        lax.cond(
-            largest[0] <= small,
-            functools.partial(solve, dims, small, 1),
-            functools.partial(solve, dims, own * CAPACITY // GROUP, 2),
-            *operands,
-        )
+    field, direction, residual, image, step = lax.cond(
+        largest[0] <= small,
+        functools.partial(solve, dims, small, 1),
+        functools.partial(solve, dims, own * CAPACITY // GROUP, 2),
+        *operands,
     )
+    return field + step * direction, residual - step * image
 
 
 def solution(mesh):

time: 66.4 us -> 61.3 us (0.923)
  Pallas kernels: 63 us -> 59.2 us
  local copies, waits for them, and re-layouts: 1.88 us -> 0.01 us
    pallas_call x1, Pallas kernels: 46.8 us -> 43.6 us  [solve(): pl.pallas_call(functools.partial(solve_kernel, dims, groups), out_shape=[...]
    unnamed x8 -> x4, local copies, waits for them, and re-layouts: 1.88 us -> 0.01 us
where the time goes in v3:
time: 61.3 us; the launch traced here: 61.1 us
  Pallas kernels  59.2 us (97%)
  between operations  1.24 us (2%)
  other arithmetic  0.62 us (1%)
    pallas_call x1, Pallas kernels, solve(): pl.pallas_call(functools.partial(solve_kernel, dims, groups), out_shape=[...  43.6 us
    pallas_call x1, Pallas kernels, all_gather(): pl.pallas_call(functools.partial(gather_kernel, dims), out_shape=[jax.Sha...  15.6 us

profile of v3, /device:TPU:0, one launch (start us, length us, event | category | flops | bytes accessed | tf_op | source)
XLA Modules:
  0.0 61.1 jit_solution(12284264753534557330)
XLA Ops:
  0.6 0.0 copy-start
  0.6 0.0 copy-start.1
  0.7 15.6 %shard_map.59 = (f32[32,8,256]{2,1,0:T(8,128)S(1)}, f32[32,2,8,256]{3,2,1,0:T(8,128)S(1)}, f32[2,256]{1,0:T(2,128)S(1)}, s32[1,128]{1,0:T(1,128)S(1)}, s32[1,128]{1,0:T(1,128)S(1)}, /*index=5*/s32[1]{0:T(128)}) custom-call(f32[3,2,256]{2,1,0:T(2,128)} %bitcast.2, f32[2,8,256]{2,1,0:T(8,128)} %guess_in.1, f32[2,256]{1,0:T(2,128)} %noise_in.1), custom_call_target="tpu_custom_call" | custom-call | tf_op jit(solution)/shard_map/pallas_call | solution.py:262
  16.8 0.0 copy-done
  16.8 0.0 copy-done.1
  16.8 43.6 %conditional.1 = ((f32[2,8,256]{2,1,0:T(8,128)S(1)}, f32[2,8,256]{2,1,0:T(8,128)S(1)}, f32[2,8,256]{2,1,0:T(8,128)S(1)}, f32[2,8,256]{2,1,0:T(8,128)S(1)}, f32[8,256]{1,0:T(8,128)S(1)})) conditional(s32[]{:T(128)} %bitcast.1, (s32[1,128]{1,0:T(1,128)S(1)}, s32[1,128]{1,0:T(1,128)S(1)}, f32[32,8,256]{2,1,0:T(8,128)S(1)}, f32[2,256]{1,0:T(2,128)S(1)}, ...), branch_computations={%region_0.0_spmd, %region_1.0_spmd} | conditional | bytes 8 | solution.py:603
  16.9 43.6 %branch_1_fun.1 = (f32[2,8,256]{2,1,0:T(8,128)S(1)}, f32[2,8,256]{2,1,0:T(8,128)S(1)}, f32[2,8,256]{2,1,0:T(8,128)S(1)}, f32[2,8,256]{2,1,0:T(8,128)S(1)}, f32[8,256]{1,0:T(8,128)S(1)}) custom-call(s32[1,128]{1,0:T(1,128)S(1)} %get-tuple-element.35.near_ref, s32[1,128]{1,0:T(1,128)S(1)} %get-tuple-element.36.side_ref, ...), custom_call_target="tpu_custom_call" | custom-call | tf_op jit(solution)/shard_map/cond/branch_1_fun/pallas_call | solution.py:568
  60.5 0.6 %multiply_subtract_fusion = (f32[2,8,256]{2,1,0:T(8,128)}, f32[2,8,256]{2,1,0:T(8,128)}) fusion(f32[2,8,256]{2,1,0:T(8,128)S(1)} %get-tuple-element.64, f32[2,8,256]{2,1,0:T(8,128)S(1)} %get-tuple-element.65, f32[8,256]{1,0:T(8,128)S(1)} %get-tuple-element.62, f32[2,8,256]{2,1,0:T(8,128)S(1)} %get-tuple-element.61, f32[2,8,256]{2,1,0:T(8,128)S(1)} %get-tuple-element.63), kind=kLoop, calls=%fused_computation | loop fusion | flops 16384 | bytes 106496 | tf_op jit(solution)/shard_map/sub | solution.py:609
Async XLA Ops:
  0.6 16.2 %copy-start = (f32[2,8,256]{2,1,0:T(8,128)S(1)}, f32[2,8,256]{2,1,0:T(8,128)}, u32[]{:S(2)}) copy-start(f32[2,8,256]{2,1,0:T(8,128)} %guess_in.1) | copy-start | bytes 49156
  0.6 16.2 %copy-start.1 = (f32[2,8,256]{2,1,0:T(8,128)S(1)}, f32[2,8,256]{2,1,0:T(8,128)}, u32[]{:S(2)}) copy-start(f32[2,8,256]{2,1,0:T(8,128)} %param.9) | copy-start | bytes 49156

commit v4 on v3

--- a/solution.py
+++ b/solution.py
@@ -42,6 +42,16 @@
         result = result + (index // bit + k // bit) % 2 * bit
         bit *= 2
     return result
+
+
+def plane_order(x, y, c):
+    return (1 - x, 1 - y), ((x + c) % 2, (y + 1 - c) % 2), ((x + 1 - c) % 2, (y + c) % 2)
+
+
+def straight(k, levels, arrays):
+    if arrays > 1 or k == 0 or k + 1 >= levels:
+        return ()
+    return (0, 1, 2)[: 3 if k == 1 else 1 if k == 2 else 0]
 
 
 def gather_partners(dims):
@@ -95,40 +105,54 @@
     mine = slot(x, z, y, c)
     other = device(x, z, y, 1 - c)
     along_z = {}
-    for k in reversed(range(1, zs)):
+    if xs == 2 and ys == 2:
+        across_by = plane_order(x, y, c)
+        last = zs - 1
+        arrivals, swaps = {}, []
+
+        def hand_on(k, a):
+            level = flip(z, k, zs)
+            if k:
+                along_z[k, a].wait_recv()
+            place = slot(x, level, y, c)
+            source = outs[a].at[place] if k else ins[a]
+            for way, (xx, yy) in enumerate(across_by):
+                if way in straight(k, zs, count):
+                    continue
+                copy = send(a, source, place, device(xx, z, yy, c))
+                arrivals[a, k, way] = (copy, slot(xx, level, yy, c))
+                if k and k == last:
+                    swaps.append((a, send(a, source, place, device(xx, z, yy, 1 - c))))
+            swaps.append((a, send(a, source, place, other)))
+
+        for k in reversed(range(1, zs)):
+            for a in range(count):
+                level = flip(z, k, zs)
+                if k > 1:
+                    along_z[k, a] = send(a, ins[a], mine, device(x, level, y, c))
+                for way in straight(k, zs, count):
+                    xx, yy = across_by[way]
+                    copy = send(a, ins[a], mine, device(xx, level, yy, c))
+                    arrivals[a, k, way] = (copy, slot(xx, level, yy, c))
+                if k == 1:
+                    along_z[k, a] = send(a, ins[a], mine, device(x, level, y, c))
         for a in range(count):
-            along_z[k, a] = send(a, ins[a], mine, device(x, flip(z, k, zs), y, c))
-    if xs == 2 and ys == 2:
-        across_by = ((1 - x, 1 - y), ((x + c) % 2, (y + 1 - c) % 2), ((x + 1 - c) % 2, (y + c) % 2))
-        arrivals, swaps = [], []
-
-        def hand_on(k):
-            level = flip(z, k, zs)
+            hand_on(0, a)
+        yield "sent"
+        for k in sorted(range(1, zs), key=lambda k: (len(straight(k, zs, count)) == 3, k)):
             for a in range(count):
-                if k:
-                    along_z[k, a].wait_recv()
-                place = slot(x, level, y, c)
-                source = outs[a].at[place] if k else ins[a]
-                for xx, yy in across_by:
-                    copy = send(a, source, place, device(xx, z, yy, c))
-                    arrivals.append((copy, a, k, slot(xx, level, yy, c)))
-                    if k == zs - 1:
-                        swaps.append((a, send(a, source, place, device(xx, z, yy, 1 - c))))
-                swaps.append((a, send(a, source, place, other)))
-
-        hand_on(0)
-        yield "sent"
-        for k in range(1, zs):
-            hand_on(k)
+                hand_on(k, a)
+        ways = (1, 2, 0)
+        early = min(zs, 2) if count == 1 else 0
+        order = [(k, way) for k in range(early) for way in ways]
+        order += [(k, way) for way in ways for k in range(early, zs)]
+        order.sort(key=lambda step: step[0] == last)
         for first in range(count):
-            for way in (1, 2, 0):
-                for copy, a, k, place in arrivals[way::3]:
-                    if a == first and k < zs - 1:
-                        copy.wait_recv()
-                        swaps.append((a, send(a, outs[a].at[place], place, other)))
-            for copy, a, k, place in arrivals:
-                if a == first and k == zs - 1:
-                    copy.wait_recv()
+            for k, way in order:
+                copy, place = arrivals[first, k, way]
+                copy.wait_recv()
+                if k == 0 or k < last:
+                    swaps.append((first, send(first, outs[first].at[place], place, other)))
         for first in range(count):
             for a, copy in swaps:
                 if a == first:
@@ -140,6 +164,9 @@
             copy.wait_send()
         return
 
+    for k in reversed(range(1, zs)):
+        for a in range(count):
+            along_z[k, a] = send(a, ins[a], mine, device(x, flip(z, k, zs), y, c))
     for copy in local:
         copy.wait()
 
@@ -312,8 +339,10 @@
     me = lax.axis_index("row") * cols + lax.axis_index("col")
 
     def peer(k):
-        number = (me + k) % devices
-        return (number // cols, number % cols)
+        number = me + k
+        number = jnp.where(number >= devices, number - devices, number)
+        row = lax.div(number, cols)
+        return (row, number - row * cols)
 
     barrier = pltpu.get_barrier_semaphore()
 
@@ -411,7 +440,7 @@
             )
 
         start = tuple(jnp.zeros((2 * rhs, tile), jnp.float32) for _ in range(own))
-        totals = lax.fori_loop(0, groups, step, start, unroll=4 if groups % 4 == 0 else 2)
+        totals = lax.fori_loop(0, groups, step, start, unroll=8 if groups % 8 == 0 else 2)
         return [(total[:rhs] + total[rhs:]) * (1.0 / 256.0) for total in totals]
 
     def over_tiles(body, start):

time: 61.3 us -> 60 us (0.979)
  Pallas kernels: 59.2 us -> 57.8 us
    pallas_call x1, Pallas kernels: 43.6 us -> 42.2 us  [solve(): pl.pallas_call(functools.partial(solve_kernel, dims, groups), out_shape=[...]
where the time goes in v4:
time: 60 us; the launch traced here: 59.8 us
  Pallas kernels  57.8 us (96%)
  between operations  1.24 us (2%)
  other arithmetic  0.62 us (1%)
    pallas_call x1, Pallas kernels, solve(): pl.pallas_call(functools.partial(solve_kernel, dims, groups), out_shape=[...  42.2 us
    pallas_call x1, Pallas kernels, all_gather(): pl.pallas_call(functools.partial(gather_kernel, dims), out_shape=[jax.Sha...  15.6 us

profile of v4, /device:TPU:0, one launch (start us, length us, event | category | flops | bytes accessed | tf_op | source)
XLA Modules:
  0.0 59.8 jit_solution(15415525444903660068)
XLA Ops:
  0.6 0.0 copy-start
  0.6 0.0 copy-start.1
  0.7 15.6 %shard_map.59 = (f32[32,8,256]{2,1,0:T(8,128)S(1)}, f32[32,2,8,256]{3,2,1,0:T(8,128)S(1)}, f32[2,256]{1,0:T(2,128)S(1)}, s32[1,128]{1,0:T(1,128)S(1)}, s32[1,128]{1,0:T(1,128)S(1)}, /*index=5*/s32[1]{0:T(128)}) custom-call(f32[3,2,256]{2,1,0:T(2,128)} %bitcast.2, f32[2,8,256]{2,1,0:T(8,128)} %guess_in.1, f32[2,256]{1,0:T(2,128)} %noise_in.1), custom_call_target="tpu_custom_call" | custom-call | tf_op jit(solution)/shard_map/pallas_call | solution.py:289
  16.8 0.0 copy-done
  16.8 0.0 copy-done.1
  16.8 42.4 %conditional.1 = ((f32[2,8,256]{2,1,0:T(8,128)S(1)}, f32[2,8,256]{2,1,0:T(8,128)S(1)}, f32[2,8,256]{2,1,0:T(8,128)S(1)}, f32[2,8,256]{2,1,0:T(8,128)S(1)}, f32[8,256]{1,0:T(8,128)S(1)})) conditional(s32[]{:T(128)} %bitcast.1, (s32[1,128]{1,0:T(1,128)S(1)}, s32[1,128]{1,0:T(1,128)S(1)}, f32[32,8,256]{2,1,0:T(8,128)S(1)}, f32[2,256]{1,0:T(2,128)S(1)}, ...), branch_computations={%region_0.0_spmd, %region_1.0_spmd} | conditional | bytes 8 | solution.py:632
  17.0 42.2 %branch_1_fun.1 = (f32[2,8,256]{2,1,0:T(8,128)S(1)}, f32[2,8,256]{2,1,0:T(8,128)S(1)}, f32[2,8,256]{2,1,0:T(8,128)S(1)}, f32[2,8,256]{2,1,0:T(8,128)S(1)}, f32[8,256]{1,0:T(8,128)S(1)}) custom-call(s32[1,128]{1,0:T(1,128)S(1)} %get-tuple-element.35.near_ref, s32[1,128]{1,0:T(1,128)S(1)} %get-tuple-element.36.side_ref, ...), custom_call_target="tpu_custom_call" | custom-call | tf_op jit(solution)/shard_map/cond/branch_1_fun/pallas_call | solution.py:597
  59.2 0.6 %multiply_subtract_fusion = (f32[2,8,256]{2,1,0:T(8,128)}, f32[2,8,256]{2,1,0:T(8,128)}) fusion(f32[2,8,256]{2,1,0:T(8,128)S(1)} %get-tuple-element.64, f32[2,8,256]{2,1,0:T(8,128)S(1)} %get-tuple-element.65, f32[8,256]{1,0:T(8,128)S(1)} %get-tuple-element.62, f32[2,8,256]{2,1,0:T(8,128)S(1)} %get-tuple-element.61, f32[2,8,256]{2,1,0:T(8,128)S(1)} %get-tuple-element.63), kind=kLoop, calls=%fused_computation | loop fusion | flops 16384 | bytes 106496 | tf_op jit(solution)/shard_map/sub | solution.py:638
Async XLA Ops:
  0.6 16.2 %copy-start = (f32[2,8,256]{2,1,0:T(8,128)S(1)}, f32[2,8,256]{2,1,0:T(8,128)}, u32[]{:S(2)}) copy-start(f32[2,8,256]{2,1,0:T(8,128)} %guess_in.1) | copy-start | bytes 49156
  0.6 16.2 %copy-start.1 = (f32[2,8,256]{2,1,0:T(8,128)S(1)}, f32[2,8,256]{2,1,0:T(8,128)}, u32[]{:S(2)}) copy-start(f32[2,8,256]{2,1,0:T(8,128)} %param.9) | copy-start | bytes 49156

commit v5 on v4

--- a/solution.py
+++ b/solution.py
@@ -8,7 +8,7 @@
 from jax.sharding import PartitionSpec as P
 
 ITERS = 3
-GROUP = 4
+GROUP = 3
 NEAR = 27
 CAPACITY = -(-NEAR // GROUP) * GROUP
 CORES = 2
@@ -216,7 +216,7 @@
         gap = jnp.maximum(low - high_row, low_row - high)
         far = gap if far is None else jnp.maximum(far, gap)
     near = jnp.where(far < 1.0, 1.0, 0.0)
-    needed = jnp.ceil(jnp.sum(near, axis=1, keepdims=True) * (1.0 / GROUP))
+    needed = jnp.ceil((jnp.sum(near, axis=1, keepdims=True) - 0.5) * (1.0 / GROUP))
     groups = sum(needed[p * devices : (p + 1) * devices] for p in range(own))
     largest_ref[0] = jnp.max(groups).astype(jnp.int32)
 
@@ -230,7 +230,7 @@
     slots = lax.broadcasted_iota(jnp.int32, (tiles, ids_ref.shape[1]), 1).astype(jnp.float32)
     place = lax.broadcasted_iota(jnp.int32, (tiles, 1), 0)
     tile_ids = (place % devices * own + place // devices + 1).astype(jnp.float32)
-    group_ids = lax.broadcasted_iota(jnp.int32, side_ref.shape, 1).astype(jnp.float32)
+    slot_ids = lax.broadcasted_iota(jnp.int32, side_ref.shape, 1).astype(jnp.float32)
     found, side = 0.0, jnp.zeros(side_ref.shape, jnp.float32)
     first = jnp.zeros((1, 1), jnp.float32)
     for p in range(own):
@@ -239,8 +239,8 @@
         goal = jnp.where(chosen > 0.0, column_of(rank, lane) + first * GROUP, -1.0)
         found = found + jnp.where(goal == slots, tile_ids, 0.0)
         if p:
-            side = side + jnp.where(group_ids >= first, 1.0, 0.0)
-        first = first + jnp.ceil(jnp.sum(chosen, axis=0, keepdims=True) * (1.0 / GROUP))
+            side = side + jnp.where(slot_ids >= first * GROUP, 1.0, 0.0)
+        first = first + jnp.ceil((jnp.sum(chosen, axis=0, keepdims=True) - 0.5) * (1.0 / GROUP))
     ids_ref[...] = (jnp.sum(found, axis=0, keepdims=True) - 1.0).astype(jnp.int32)
     side_ref[...] = side.astype(jnp.int32)
 
@@ -389,7 +389,7 @@
 
     def measure(e, target):
         near = jnp.maximum(near_ref[0, e], 0)
-        p = side_ref[0, e // GROUP]
+        p = side_ref[0, e]
         points = jnp.where(line < 3, place_points(near // own, near % own) - centers[p], 0.0)
         squares = jnp.sum(points * points, axis=0, keepdims=True)
         value = jnp.where(line == 3, squares, jnp.where(line == 4, 1.0, points))
@@ -433,14 +433,14 @@
                 blocks[pl.ds(first, GROUP * block), :],
                 preferred_element_type=jnp.float32,
             )
-            place = side_ref[0, g].astype(jnp.float32)
+            place = side_ref[0, g * GROUP].astype(jnp.float32)
             return tuple(
                 total + term * jnp.maximum(1.0 - jnp.abs(place - float(p)), 0.0)
                 for p, total in enumerate(totals)
             )
 
         start = tuple(jnp.zeros((2 * rhs, tile), jnp.float32) for _ in range(own))
-        totals = lax.fori_loop(0, groups, step, start, unroll=8 if groups % 8 == 0 else 2)
+        totals = lax.fori_loop(0, groups, step, start, unroll=10 if groups % 10 == 0 else 2)
         return [(total[:rhs] + total[rhs:]) * (1.0 / 256.0) for total in totals]
 
     def over_tiles(body, start):
@@ -456,7 +456,7 @@
         return [jnp.sum(total, axis=1, keepdims=True) for total in over_tiles(body, start)]
 
     measure(0, squared0)
-    lax.fori_loop(0, groups * GROUP // 2, build, 0, unroll=4)
+    lax.fori_loop(0, groups * GROUP // 2, build, 0, unroll=5 if groups % 5 == 0 else 1)
     noise = [noise_ref[p : p + 1, :] for p in range(own)]
     pl.semaphore_wait(barrier, devices - 1)
 
@@ -628,7 +628,7 @@
     gathered = all_gather(dims, 0, placed, start_guess, noise_var)
     points, guesses, noise, near_ids, side, largest = gathered
     operands = (near_ids, side, points, noise, right_side, start_guess, guesses)
-    small = own * 4
+    small = own * 5
     field, direction, residual, image, step = lax.cond(
         largest[0] <= small,
         functools.partial(solve, dims, small, 1),

time: 60 us -> 59.5 us (level)
  no operation moved by 1% of the time
where the time goes in v5:
time: 59.5 us; the launch traced here: 59.3 us
  Pallas kernels  57.2 us (96%)
  between operations  1.24 us (2%)
  other arithmetic  0.62 us (1%)
    pallas_call x1, Pallas kernels, solve(): pl.pallas_call(functools.partial(solve_kernel, dims, groups), out_shape=[...  41.6 us
    pallas_call x1, Pallas kernels, all_gather(): pl.pallas_call(functools.partial(gather_kernel, dims), out_shape=[jax.Sha...  15.6 us

profile of v5, /device:TPU:0, one launch (start us, length us, event | category | flops | bytes accessed | tf_op | source)
XLA Modules:
  0.0 59.3 jit_solution(4340135499067920029)
XLA Ops:
  0.6 0.0 copy-start
  0.6 0.0 copy-start.1
  0.7 15.6 %shard_map.59 = (f32[32,8,256]{2,1,0:T(8,128)S(1)}, f32[32,2,8,256]{3,2,1,0:T(8,128)S(1)}, f32[2,256]{1,0:T(2,128)S(1)}, s32[1,128]{1,0:T(1,128)S(1)}, s32[1,128]{1,0:T(1,128)S(1)}, /*index=5*/s32[1]{0:T(128)}) custom-call(f32[3,2,256]{2,1,0:T(2,128)} %bitcast.2, f32[2,8,256]{2,1,0:T(8,128)} %guess_in.1, f32[2,256]{1,0:T(2,128)} %noise_in.1), custom_call_target="tpu_custom_call" | custom-call | tf_op jit(solution)/shard_map/pallas_call | solution.py:289
  16.8 0.0 copy-done
  16.8 0.0 copy-done.1
  16.8 41.8 %conditional.1 = ((f32[2,8,256]{2,1,0:T(8,128)S(1)}, f32[2,8,256]{2,1,0:T(8,128)S(1)}, f32[2,8,256]{2,1,0:T(8,128)S(1)}, f32[2,8,256]{2,1,0:T(8,128)S(1)}, f32[8,256]{1,0:T(8,128)S(1)})) conditional(s32[]{:T(128)} %bitcast.1, (s32[1,128]{1,0:T(1,128)S(1)}, s32[1,128]{1,0:T(1,128)S(1)}, f32[32,8,256]{2,1,0:T(8,128)S(1)}, f32[2,256]{1,0:T(2,128)S(1)}, ...), branch_computations={%region_0.0_spmd, %region_1.0_spmd} | conditional | bytes 8 | solution.py:632
  17.0 41.6 %branch_1_fun.1 = (f32[2,8,256]{2,1,0:T(8,128)S(1)}, f32[2,8,256]{2,1,0:T(8,128)S(1)}, f32[2,8,256]{2,1,0:T(8,128)S(1)}, f32[2,8,256]{2,1,0:T(8,128)S(1)}, f32[8,256]{1,0:T(8,128)S(1)}) custom-call(s32[1,128]{1,0:T(1,128)S(1)} %get-tuple-element.35.near_ref, s32[1,128]{1,0:T(1,128)S(1)} %get-tuple-element.36.side_ref, ...), custom_call_target="tpu_custom_call" | custom-call | tf_op jit(solution)/shard_map/cond/branch_1_fun/pallas_call | solution.py:597
  58.7 0.6 %multiply_subtract_fusion = (f32[2,8,256]{2,1,0:T(8,128)}, f32[2,8,256]{2,1,0:T(8,128)}) fusion(f32[2,8,256]{2,1,0:T(8,128)S(1)} %get-tuple-element.64, f32[2,8,256]{2,1,0:T(8,128)S(1)} %get-tuple-element.65, f32[8,256]{1,0:T(8,128)S(1)} %get-tuple-element.62, f32[2,8,256]{2,1,0:T(8,128)S(1)} %get-tuple-element.61, f32[2,8,256]{2,1,0:T(8,128)S(1)} %get-tuple-element.63), kind=kLoop, calls=%fused_computation | loop fusion | flops 16384 | bytes 106496 | tf_op jit(solution)/shard_map/sub | solution.py:638
Async XLA Ops:
  0.6 16.2 %copy-start = (f32[2,8,256]{2,1,0:T(8,128)S(1)}, f32[2,8,256]{2,1,0:T(8,128)}, u32[]{:S(2)}) copy-start(f32[2,8,256]{2,1,0:T(8,128)} %guess_in.1) | copy-start | bytes 49156
  0.6 16.2 %copy-start.1 = (f32[2,8,256]{2,1,0:T(8,128)S(1)}, f32[2,8,256]{2,1,0:T(8,128)}, u32[]{:S(2)}) copy-start(f32[2,8,256]{2,1,0:T(8,128)} %param.9) | copy-start | bytes 49156
